TPU v7x, 256 devices: a whole 4x4x8 slice. The times are simulated.
256 devices in a mesh: gx: 32 (over y_hi, z, core), gy: 8 (over y_lo, x).
Axes of the slice: x: 4, y: 4 (y_hi: 2, y_lo: 2; y = y_hi * 2 + y_lo), z: 8, core: 2. Of those that a mesh axis runs over, the one named last changes fastest.
Arguments:
- adj_later: float32 [19, 256, 128, 256], P(None, 'gx', 'gy'), may hold values from -6 to 6
- saved_pops: bfloat16 [2, 19, 256, 128, 256], P(None, None, 'gx', 'gy'), may hold values from 0.015 to 0.49, as said below
- saved_scale: float32 [2, 19, 256, 128, 2], P(None, None, 'gx', 'gy'), may hold values from 0.7 to 1.4
- solid: int32 [256, 128, 256], P('gx', 'gy'), may hold values 0 or 1
- seed_values: float32 [32768, 19], P(('gx', 'gy')), may hold values from -12 to 12
- seed_contact: int32 [32768, 1], P(('gx', 'gy')), may hold values from 0 to 8; in each aligned block of 128 rows (0 to 127, 128 to 255, ...) at most 32 rows name the same one
- seed_cell: int32 [32768], P(('gx', 'gy')), may hold values from 0 to 32767
Outputs:
- adj_initial: float32 [19, 256, 128, 256], P(None, 'gx', 'gy')
- adj_middle: float32 [19, 256, 128, 256], P(None, 'gx', 'gy')
Inputs may be any that keep to these rules, and one draw needn't show every extreme that they name: `saved_pops`: each saved population is its lattice weight w_i times a factor between 0.55 and 1.45. `seed_contact`: among the items held by one device no contact code appears more than 32 times; some code reaches 32 on some device.
All inputs are finite; a program needn't handle non-finite values. No bound on the sum of `solid` on one device may be relied on, other than what follows from the above.
Results may differ from a plain program's by a relative error of at most 0.0003.
Values sent between devices are 32-bit elements; how exact they have to be, the bound alone decides.
No kernel may reach another device: no remote copies, remote signals or barrier semaphores. Data moves between devices by JAX's collectives and lax.ppermute only.
A program may use at most 128 MiB of HBM per device.

v0:
```python
import jax
import jax.numpy as jnp
from jax import lax
from jax.sharding import PartitionSpec as P

LATTICE = [
    (0, 0, 0),
    (1, 0, 0),
    (-1, 0, 0),
    (0, 1, 0),
    (0, -1, 0),
    (0, 0, 1),
    (0, 0, -1),
    (1, 1, 0),
    (-1, -1, 0),
    (1, -1, 0),
    (-1, 1, 0),
    (1, 0, 1),
    (-1, 0, -1),
    (1, 0, -1),
    (-1, 0, 1),
    (0, 1, 1),
    (0, -1, -1),
    (0, 1, -1),
    (0, -1, 1),
]
OPPOSITE = [0, 2, 1, 4, 3, 6, 5, 8, 7, 10, 9, 12, 11, 14, 13, 16, 15, 18, 17]
LATTICE_WEIGHTS = [1.0 / 3.0] + [1.0 / 18.0] * 6 + [1.0 / 36.0] * 12
relaxation = 0.8


def padded(cells, sides, width):
    for axis, dim in sides:
        count = lax.axis_size(axis)
        ends = count - 1
        head = lax.slice_in_dim(cells, 0, width, axis=dim)
        tail = lax.slice_in_dim(cells, cells.shape[dim] - width, cells.shape[dim], axis=dim)
        cells = jnp.concatenate(
            [
                lax.ppermute(tail, axis, [(i, (i + 1) % count) for i in range(ends)]),
                cells,
                lax.ppermute(head, axis, [((i + 1) % count, i) for i in range(ends)]),
            ],
            axis=dim,
        )
    return cells


def adjoint_collide(populations, read, solid):
    pops_list = [populations[index] for index in range(19)]
    density = pops_list[0]
    for index in range(1, 19):
        density = density + pops_list[index]
    momenta = []
    for axis_pos in range(3):
        total = jnp.zeros_like(density)
        for index in range(19):
            factor = LATTICE[index][axis_pos]
            if factor == 1:
                total = total + pops_list[index]
            elif factor == -1:
                total = total - pops_list[index]
        momenta.append(total)
    velocity = [momentum / density for momentum in momenta]
    square = velocity[0] * velocity[0] + velocity[1] * velocity[1] + velocity[2] * velocity[2]
    grad_density = jnp.zeros_like(density)
    weight_total = jnp.zeros_like(density)
    grad_moment = [jnp.zeros_like(density) for axis_pos in range(3)]
    for index in range(19):
        weighted = LATTICE_WEIGHTS[index] * read[index]
        weight_total = weight_total + weighted
        projected = jnp.zeros_like(density)
        for axis_pos in range(3):
            factor = LATTICE[index][axis_pos]
            if factor != 0:
                projected = projected + factor * velocity[axis_pos]
        grad_density = grad_density + weighted * (1.0 - 4.5 * projected * projected + 1.5 * square)
        linear = 3.0 * weighted * (1.0 + 3.0 * projected)
        for axis_pos in range(3):
            factor = LATTICE[index][axis_pos]
            if factor != 0:
                grad_moment[axis_pos] = grad_moment[axis_pos] + factor * linear
    grad_moment = [
        grad_moment[axis_pos] - 3.0 * weight_total * velocity[axis_pos] for axis_pos in range(3)
    ]
    is_solid = solid > 0
    results = []
    for index in range(19):
        inner = grad_density
        for axis_pos in range(3):
            factor = LATTICE[index][axis_pos]
            if factor != 0:
                inner = inner + factor * grad_moment[axis_pos]
        fluid_value = (1.0 - 1.0 / relaxation) * read[index] + inner / relaxation
        results.append(jnp.where(is_solid, read[OPPOSITE[index]], fluid_value))
    return jnp.stack(results)


def dequantize(quantized, scales):
    channels, width_x, width_y, height = quantized.shape
    blocks = quantized.astype(jnp.float32).reshape(channels, width_x, width_y, scales.shape[-1], -1)
    return (blocks * scales[..., None]).reshape(channels, width_x, width_y, height)


def shift_height(field, step_z):
    if step_z == 1:
        return jnp.concatenate([field[..., 1:], jnp.zeros_like(field[..., :1])], -1)
    if step_z == -1:
        return jnp.concatenate([jnp.zeros_like(field[..., :1]), field[..., :-1]], -1)
    return field


def stream_back(adjoint):
    width_x, width_y = (adjoint.shape[1], adjoint.shape[2])
    read = []
    extended = padded(adjoint, (("gx", 1), ("gy", 2)), 1)
    for direction in range(19):
        step_x, step_y, step_z = LATTICE[direction]
        plane = extended[
            direction, 1 + step_x : 1 + step_x + width_x, 1 + step_y : 1 + step_y + width_y
        ]
        read.append(shift_height(plane, step_z))
    return read


def deliver_seeds(seed_values, seed_contact, seed_cell, cell_count):
    surf_dev = seed_values.shape[0]
    contact = seed_contact[:, 0]
    empty_field = jnp.zeros((19, cell_count), jnp.float32)
    labels = (contact * cell_count + seed_cell).astype(jnp.float32)
    payload = jnp.concatenate([seed_values, labels[:, None]], 1).reshape(1, 1, surf_dev, 20)
    nearby = padded(payload, (("gx", 0), ("gy", 1)), 1)
    label_int = nearby[..., 19].astype(jnp.int32)
    code_int = label_int // cell_count
    target_cell = (label_int % cell_count).reshape(-1)
    row_pos = jnp.arange(3, dtype=jnp.int32)
    wanted = 8 - 3 * row_pos[:, None, None] - row_pos[None, :, None]
    matched = (code_int == wanted).astype(jnp.float32)
    values = (nearby[..., :19] * matched[..., None]).reshape(-1, 19)
    return empty_field.at[:, target_cell].add(values.T)


def body(adj_later, saved_pops, saved_scale, solid, seed_values, seed_contact, seed_cell):
    channels, width_x, width_y, height = adj_later.shape
    cell_count = width_x * width_y * height
    seed_field = deliver_seeds(seed_values, seed_contact, seed_cell, cell_count)
    adjoint_end = adj_later + seed_field.reshape(channels, width_x, width_y, height)
    pops_late = dequantize(saved_pops[1], saved_scale[1])
    adj_middle = adjoint_collide(pops_late, stream_back(adjoint_end), solid)
    pops_early = dequantize(saved_pops[0], saved_scale[0])
    adj_initial = adjoint_collide(pops_early, stream_back(adj_middle), solid)
    return (adj_initial, adj_middle)


def solution(mesh):
    return jax.shard_map(
        body,
        mesh=mesh,
        in_specs=(
            P(None, "gx", "gy", None),
            P(None, None, "gx", "gy", None),
            P(None, None, "gx", "gy", None),
            P("gx", "gy", None),
            P(("gx", "gy"), None),
            P(("gx", "gy"), None),
            P(("gx", "gy")),
        ),
        out_specs=(P(None, "gx", "gy", None), P(None, "gx", "gy", None)),
        check_vma=False,
    )
```

profile of v0, /device:TPU:24, one launch (start us, length us, event | category | flops | bytes accessed | tf_op | source)
XLA Modules:
  0.0 193.3 jit_solution(471133814534400628)
XLA Ops:
  2.0 2.0 %collective-permute-start = (f32[1,1,128,20]{2,3,1,0:T(8,128)S(1)}, f32[1,1,128,20]{2,3,1,0:T(8,128)S(1)}, u32[]{:S(2)}, u32[]{:S(2)}) collective-permute-start(f32[1,1,128,20]{2,3,1,0:T(8,128)S(1)} %maximum_bitcast_fusion.24), channel_id=1, source_target_pairs={{0,8},{8,16},{16,24},{24,32},{32,40},{40,48},{48,56},{56,64},{64,7... | collective-permute-start | bytes 30728 | tf_op jit(solution)/shard_map/ppermute | solution.py:40
  4.1 7.9 %collective-permute-start.1 = (f32[1,1,128,20]{2,3,1,0:T(8,128)S(1)}, f32[1,1,128,20]{2,3,1,0:T(8,128)S(1)}, u32[]{:S(2)}, u32[]{:S(2)}) collective-permute-start(f32[1,1,128,20]{2,3,1,0:T(8,128)S(1)} %maximum_bitcast_fusion.24), channel_id=1, source_target_pairs={{8,0},{16,8},{24,16},{32,24},{40,32},{48,40},{56,48},{64,56},{72,6... | collective-permute-start | bytes 30728 | tf_op jit(solution)/shard_map/ppermute | solution.py:42
  12.0 3.8 %slice_convert_fusion = (f32[1,19,8,16,256]{4,3,2,1,0:T(8,128)}, f32[1,19,8,16,256]{4,3,2,1,0:T(8,128)S(1)}) fusion(bf16[2,19,8,16,256]{4,3,2,1,0:T(8,128)(2,1)} %param.8), kind=kLoop, calls=%fused_computation.4 | loop fusion | flops 1245184 | bytes 7471104 | tf_op jit(solution)/shard_map/convert_element_type | solution.py:101
  16.5 3.4 %collective-permute-start.2 = (f32[3,1,128,20]{2,3,1,0:T(8,128)S(1)}, f32[3,1,128,20]{2,3,1,0:T(8,128)S(1)}, u32[]{:S(2)}, u32[]{:S(2)}) collective-permute-start(f32[3,1,128,20]{2,3,1,0:T(8,128)S(1)} %pad_maximum_fusion.26), channel_id=1, source_target_pairs={{0,1},{1,2},{2,3},{3,4},{4,5},{5,6},{6,7},{8,9},{9,10},{10,11},{11... | collective-permute-start | bytes 92168 | tf_op jit(solution)/shard_map/ppermute | solution.py:40
  19.9 4.6 %collective-permute-start.3 = (f32[3,1,128,20]{2,3,1,0:T(8,128)S(1)}, f32[3,1,128,20]{2,3,1,0:T(8,128)S(1)}, u32[]{:S(2)}, u32[]{:S(2)}) collective-permute-start(f32[3,1,128,20]{2,3,1,0:T(8,128)S(1)} %pad_maximum_fusion.26), channel_id=1, source_target_pairs={{1,0},{2,1},{3,2},{4,3},{5,4},{6,5},{7,6},{9,8},{10,9},{11,10},{12... | collective-permute-start | bytes 92168 | tf_op jit(solution)/shard_map/ppermute | solution.py:42
  24.5 2.3 %reshape.193 = f32[19,8,16,2,128]{4,3,2,1,0:T(2,128)} reshape(f32[1,19,8,16,256]{4,3,2,1,0:T(8,128)S(1)} %get-tuple-element.97) | data formatting | bytes 4980736 | tf_op jit(solution)/shard_map/convert_element_type | solution.py:101
  26.8 2.2 %copy.34 = f32[19,8,16,2]{3,2,1,0:T(8,128)} copy(f32[19,8,16,2]{0,3,2,1:T(2,128)S(1)} %get-tuple-element.126) | data formatting | bytes 38912 | tf_op jit(solution)/shard_map/mul | solution.py:102
  29.5 15.6 %scatter_custom_fusion = f32[19,32768]{0,1:T(8,128)} fusion(s32[1152]{0:T(1024)S(1)} %fusion.138, f32[1152,19]{1,0:T(8,128)S(1)} %bitcast.260, f32[]{:T(128)} %constant.127.clone.1), kind=kCustom, calls=%fused_computation.1 | custom fusion | flops 21888 | bytes 2490372 | tf_op jit(solution)/shard_map/scatter-add | solution.py:140
  45.2 11.3 %copy.33 = f32[19,8,16,256]{3,2,1,0:T(8,128)} copy(f32[19,8,16,256]{0,3,2,1:T(8,128)} %bitcast.207) | data formatting | bytes 4980736 | tf_op jit(solution)/shard_map/reshape | solution.py:147
  56.4 3.2 %add.1182 = f32[19,8,16,256]{3,2,1,0:T(8,128)S(1)} add(f32[19,8,16,256]{3,2,1,0:T(8,128)} %param.7, f32[19,8,16,256]{3,2,1,0:T(8,128)} %copy.33) | non-fusion elementwise | flops 622592 | bytes 7471104 | tf_op jit(solution)/shard_map/add | solution.py:147
  60.6 3.5 %collective-permute-start.4 = (f32[19,1,16,256]{3,2,1,0:T(8,128)}, f32[19,1,16,256]{3,2,1,0:T(8,128)S(1)}, u32[]{:S(2)}, u32[]{:S(2)}) collective-permute-start(f32[19,1,16,256]{3,2,1,0:T(8,128)} %get-tuple-element.124), channel_id=1, source_target_pairs={{8,0},{16,8},{24,16},{32,24},{40,32},{48,40},{56,48},{64,56},{72,6... | collective-permute-start | bytes 933896 | tf_op jit(solution)/shard_map/ppermute | solution.py:42
  64.1 2.1 %collective-permute-start.5 = (f32[19,1,16,256]{3,2,1,0:T(8,128)}, f32[19,1,16,256]{3,2,1,0:T(8,128)S(1)}, u32[]{:S(2)}, u32[]{:S(2)}) collective-permute-start(f32[19,1,16,256]{3,2,1,0:T(8,128)} %get-tuple-element.123), channel_id=1, source_target_pairs={{0,8},{8,16},{16,24},{24,32},{32,40},{40,48},{48,56},{56,64},{64,7... | collective-permute-start | bytes 933896 | tf_op jit(solution)/shard_map/ppermute | solution.py:40
  66.3 2.9 %broadcast_multiply_fusion.1 = f32[19,8,16,2,128]{4,3,2,1,0:T(2,128)S(1)} fusion(f32[19,8,16,2,128]{4,3,2,1,0:T(2,128)S(1)} %copy-done.3, f32[19,8,16,2]{3,2,1,0:T(8,128)S(1)} %copy-done.5), kind=kLoop, calls=%fused_computation.5 | loop fusion | flops 622592 | bytes 5000192 | tf_op jit(solution)/shard_map/mul | solution.py:102
  99.6 4.0 %reshape.194 = f32[19,8,16,2,128]{4,3,2,1,0:T(2,128)} reshape(f32[1,19,8,16,256]{4,3,2,1,0:T(8,128)} %get-tuple-element.96) | data formatting | bytes 4980736 | tf_op jit(solution)/shard_map/convert_element_type | solution.py:101
  103.7 2.3 %copy.35 = f32[19,8,16,2]{3,2,1,0:T(8,128)} copy(f32[19,8,16,2]{0,3,2,1:T(2,128)S(1)} %copy-done.42) | data formatting | bytes 38912 | tf_op jit(solution)/shard_map/mul | solution.py:102
  106.2 2.1 %collective-permute-start.6 = (f32[19,10,1,256]{3,2,1,0:T(1,128)S(1)}, f32[19,10,1,256]{3,2,1,0:T(1,128)S(1)}, u32[]{:S(2)}, u32[]{:S(2)}) collective-permute-start(f32[19,10,1,256]{3,2,1,0:T(1,128)S(1)} %get-tuple-element.69), channel_id=1, source_target_pairs={{1,0},{2,1},{3,2},{4,3},{5,4},{6,5},{7,6},{9,8},{10,9},{11,10},{12... | collective-permute-start | bytes 583688 | tf_op jit(solution)/shard_map/ppermute | solution.py:42
  108.4 3.7 %collective-permute-start.7 = (f32[19,10,1,256]{3,2,1,0:T(1,128)S(1)}, f32[19,10,1,256]{3,2,1,0:T(1,128)S(1)}, u32[]{:S(2)}, u32[]{:S(2)}) collective-permute-start(f32[19,10,1,256]{3,2,1,0:T(1,128)S(1)} %get-tuple-element.70), channel_id=1, source_target_pairs={{0,1},{1,2},{2,3},{3,4},{4,5},{5,6},{6,7},{8,9},{9,10},{10,11},{11... | collective-permute-start | bytes 583688 | tf_op jit(solution)/shard_map/ppermute | solution.py:40
  113.8 5.1 %collective-permute-done.7 = f32[19,10,1,256]{3,2,1,0:T(1,128)S(1)} collective-permute-done((f32[19,10,1,256]{3,2,1,0:T(1,128)S(1)}, f32[19,10,1,256]{3,2,1,0:T(1,128)S(1)}, u32[]{:S(2)}, u32[]{:S(2)}) %collective-permute-start.7) | collective-permute-done | bytes 194592 | tf_op jit(solution)/shard_map/ppermute | solution.py:40
  124.0 5.8 %collective-permute-start.8 = (f32[19,1,16,256]{3,2,1,0:T(8,128)S(1)}, f32[19,1,16,256]{3,2,1,0:T(8,128)S(1)}, u32[]{:S(2)}, u32[]{:S(2)}) collective-permute-start(f32[19,1,16,256]{3,2,1,0:T(8,128)S(1)} %get-tuple-element.100), channel_id=1, source_target_pairs={{8,0},{16,8},{24,16},{32,24},{40,32},{48,40},{56,48},{64,56},{72,6... | collective-permute-start | bytes 933896 | tf_op jit(solution)/shard_map/ppermute | solution.py:42
  129.9 1.9 collective-permute-start.9
  131.8 2.9 %broadcast_multiply_fusion = f32[19,8,16,2,128]{4,3,2,1,0:T(2,128)S(1)} fusion(f32[19,8,16,2,128]{4,3,2,1,0:T(2,128)S(1)} %copy-done.2, f32[19,8,16,2]{3,2,1,0:T(8,128)S(1)} %copy-done.4), kind=kLoop, calls=%fused_computation.3 | loop fusion | flops 622592 | bytes 5000192 | tf_op jit(solution)/shard_map/mul | solution.py:102
  134.7 7.0 %collective-permute-done.9 = f32[19,1,16,256]{3,2,1,0:T(8,128)S(1)} collective-permute-done((f32[19,1,16,256]{3,2,1,0:T(8,128)S(1)}, f32[19,1,16,256]{3,2,1,0:T(8,128)S(1)}, u32[]{:S(2)}, u32[]{:S(2)}) %collective-permute-start.9) | collective-permute-done | bytes 311328 | tf_op jit(solution)/shard_map/ppermute | solution.py:40
  145.3 6.3 %collective-permute-start.10 = (f32[19,10,1,256]{3,2,1,0:T(1,128)}, f32[19,10,1,256]{3,2,1,0:T(1,128)}, u32[]{:S(2)}, u32[]{:S(2)}) collective-permute-start(f32[19,10,1,256]{3,2,1,0:T(1,128)} %get-tuple-element.65), channel_id=1, source_target_pairs={{1,0},{2,1},{3,2},{4,3},{5,4},{6,5},{7,6},{9,8},{10,9},{11,10},{12... | collective-permute-start | bytes 583688 | tf_op jit(solution)/shard_map/ppermute | solution.py:42
  187.1 2.0 %bitcast_dynamic-update-slice_fusion.18 = (f32[19,8,16,256]{3,2,1,0:T(8,128)S(1)}, f32[8,16,256]{2,1,0:T(8,128)S(1)}, f32[8,16,256]{2,1,0:T(8,128)S(1)}, f32[8,1...) fusion(pred[8,16,256]{2,1,0:T(8,128)(4,1)S(1)} %get-tuple-eleme, ...), kind=kLoop, calls=%fused_computation.238 | loop fusion | flops 7274495 | bytes 9165824
  (211 shorter events, 83.4 us)
Async XLA Ops:
  2.0 13.7 %copy-start.43 = (f32[2,19,8,16,2]{1,4,3,2,0:T(2,128)S(1)}, f32[2,19,8,16,2]{1,4,3,2,0:T(2,128)}, u32[]{:S(2)}) copy-start(f32[2,19,8,16,2]{1,4,3,2,0:T(2,128)} %param.9) | copy-start | bytes 116740
  2.0 14.4 %collective-permute-start = (f32[1,1,128,20]{2,3,1,0:T(8,128)S(1)}, f32[1,1,128,20]{2,3,1,0:T(8,128)S(1)}, u32[]{:S(2)}, u32[]{:S(2)}) collective-permute-start(f32[1,1,128,20]{2,3,1,0:T(8,128)S(1)} %maximum_bitcast_fusion.24), channel_id=1, source_target_pairs={{0,8},{8,16},{16,24},{24,32},{32,40},{40,48},{48,56},{56,64},{64,7... | collective-permute-start | bytes 30728 | tf_op jit(solution)/shard_map/ppermute | solution.py:40
  4.1 12.4 %collective-permute-start.1 = (f32[1,1,128,20]{2,3,1,0:T(8,128)S(1)}, f32[1,1,128,20]{2,3,1,0:T(8,128)S(1)}, u32[]{:S(2)}, u32[]{:S(2)}) collective-permute-start(f32[1,1,128,20]{2,3,1,0:T(8,128)S(1)} %maximum_bitcast_fusion.24), channel_id=1, source_target_pairs={{8,0},{16,8},{24,16},{32,24},{40,32},{48,40},{56,48},{64,56},{72,6... | collective-permute-start | bytes 30728 | tf_op jit(solution)/shard_map/ppermute | solution.py:42
  16.5 12.6 %collective-permute-start.2 = (f32[3,1,128,20]{2,3,1,0:T(8,128)S(1)}, f32[3,1,128,20]{2,3,1,0:T(8,128)S(1)}, u32[]{:S(2)}, u32[]{:S(2)}) collective-permute-start(f32[3,1,128,20]{2,3,1,0:T(8,128)S(1)} %pad_maximum_fusion.26), channel_id=1, source_target_pairs={{0,1},{1,2},{2,3},{3,4},{4,5},{5,6},{6,7},{8,9},{9,10},{10,11},{11... | collective-permute-start | bytes 92168 | tf_op jit(solution)/shard_map/ppermute | solution.py:40
  19.9 9.2 %collective-permute-start.3 = (f32[3,1,128,20]{2,3,1,0:T(8,128)S(1)}, f32[3,1,128,20]{2,3,1,0:T(8,128)S(1)}, u32[]{:S(2)}, u32[]{:S(2)}) collective-permute-start(f32[3,1,128,20]{2,3,1,0:T(8,128)S(1)} %pad_maximum_fusion.26), channel_id=1, source_target_pairs={{1,0},{2,1},{3,2},{4,3},{5,4},{6,5},{7,6},{9,8},{10,9},{11,10},{12... | collective-permute-start | bytes 92168 | tf_op jit(solution)/shard_map/ppermute | solution.py:42
  56.4 9.8 %copy-start.3 = (f32[19,8,16,2,128]{4,3,2,1,0:T(2,128)S(1)}, f32[19,8,16,2,128]{4,3,2,1,0:T(2,128)}, u32[]{:S(2)}) copy-start(f32[19,8,16,2,128]{4,3,2,1,0:T(2,128)} %reshape.193) | copy-start | bytes 7471108
  56.4 9.8 %copy-start.5 = (f32[19,8,16,2]{3,2,1,0:T(8,128)S(1)}, f32[19,8,16,2]{3,2,1,0:T(8,128)}, u32[]{:S(2)}) copy-start(f32[19,8,16,2]{3,2,1,0:T(8,128)} %copy.34) | copy-start | bytes 58372
  60.6 45.4 %collective-permute-start.4 = (f32[19,1,16,256]{3,2,1,0:T(8,128)}, f32[19,1,16,256]{3,2,1,0:T(8,128)S(1)}, u32[]{:S(2)}, u32[]{:S(2)}) collective-permute-start(f32[19,1,16,256]{3,2,1,0:T(8,128)} %get-tuple-element.124), channel_id=1, source_target_pairs={{8,0},{16,8},{24,16},{32,24},{40,32},{48,40},{56,48},{64,56},{72,6... | collective-permute-start | bytes 933896 | tf_op jit(solution)/shard_map/ppermute | solution.py:42
  64.1 41.8 %collective-permute-start.5 = (f32[19,1,16,256]{3,2,1,0:T(8,128)}, f32[19,1,16,256]{3,2,1,0:T(8,128)S(1)}, u32[]{:S(2)}, u32[]{:S(2)}) collective-permute-start(f32[19,1,16,256]{3,2,1,0:T(8,128)} %get-tuple-element.123), channel_id=1, source_target_pairs={{0,8},{8,16},{16,24},{24,32},{32,40},{40,48},{48,56},{56,64},{64,7... | collective-permute-start | bytes 933896 | tf_op jit(solution)/shard_map/ppermute | solution.py:40
  106.2 7.5 %collective-permute-start.6 = (f32[19,10,1,256]{3,2,1,0:T(1,128)S(1)}, f32[19,10,1,256]{3,2,1,0:T(1,128)S(1)}, u32[]{:S(2)}, u32[]{:S(2)}) collective-permute-start(f32[19,10,1,256]{3,2,1,0:T(1,128)S(1)} %get-tuple-element.69), channel_id=1, source_target_pairs={{1,0},{2,1},{3,2},{4,3},{5,4},{6,5},{7,6},{9,8},{10,9},{11,10},{12... | collective-permute-start | bytes 583688 | tf_op jit(solution)/shard_map/ppermute | solution.py:42
  108.4 10.5 %collective-permute-start.7 = (f32[19,10,1,256]{3,2,1,0:T(1,128)S(1)}, f32[19,10,1,256]{3,2,1,0:T(1,128)S(1)}, u32[]{:S(2)}, u32[]{:S(2)}) collective-permute-start(f32[19,10,1,256]{3,2,1,0:T(1,128)S(1)} %get-tuple-element.70), channel_id=1, source_target_pairs={{0,1},{1,2},{2,3},{3,4},{4,5},{5,6},{6,7},{8,9},{9,10},{10,11},{11... | collective-permute-start | bytes 583688 | tf_op jit(solution)/shard_map/ppermute | solution.py:40
  112.3 6.8 %copy-start.6 = (f32[8,16,256]{2,1,0:T(8,128)S(1)}, f32[8,16,256]{2,1,0:T(8,128)}, u32[]{:S(2)}) copy-start(f32[8,16,256]{2,1,0:T(8,128)} %squeeze.225) | copy-start | bytes 393220
  112.4 6.8 %copy-start.7 = (f32[8,16,256]{2,1,0:T(8,128)S(1)}, f32[8,16,256]{2,1,0:T(8,128)}, u32[]{:S(2)}) copy-start(f32[8,16,256]{2,1,0:T(8,128)} %squeeze.226) | copy-start | bytes 393220
  112.4 6.8 %copy-start.8 = (f32[8,16,256]{2,1,0:T(8,128)S(1)}, f32[8,16,256]{2,1,0:T(8,128)}, u32[]{:S(2)}) copy-start(f32[8,16,256]{2,1,0:T(8,128)} %squeeze.227) | copy-start | bytes 393220
  112.4 6.8 %copy-start.9 = (f32[8,16,256]{2,1,0:T(8,128)S(1)}, f32[8,16,256]{2,1,0:T(8,128)}, u32[]{:S(2)}) copy-start(f32[8,16,256]{2,1,0:T(8,128)} %squeeze.228) | copy-start | bytes 393220
  112.4 6.8 %copy-start.10 = (f32[8,16,256]{2,1,0:T(8,128)S(1)}, f32[8,16,256]{2,1,0:T(8,128)}, u32[]{:S(2)}) copy-start(f32[8,16,256]{2,1,0:T(8,128)} %squeeze.229) | copy-start | bytes 393220
  123.4 8.4 %copy-start.2 = (f32[19,8,16,2,128]{4,3,2,1,0:T(2,128)S(1)}, f32[19,8,16,2,128]{4,3,2,1,0:T(2,128)}, u32[]{:S(2)}) copy-start(f32[19,8,16,2,128]{4,3,2,1,0:T(2,128)} %reshape.194) | copy-start | bytes 7471108
  123.4 8.4 %copy-start.4 = (f32[19,8,16,2]{3,2,1,0:T(8,128)S(1)}, f32[19,8,16,2]{3,2,1,0:T(8,128)}, u32[]{:S(2)}) copy-start(f32[19,8,16,2]{3,2,1,0:T(8,128)} %copy.35) | copy-start | bytes 58372
  124.0 17.7 %copy-start = (f32[19,8,16,256]{3,2,1,0:T(8,128)}, f32[19,8,16,256]{3,2,1,0:T(8,128)S(1)}, u32[]{:S(2)}) copy-start(f32[19,8,16,256]{3,2,1,0:T(8,128)S(1)} %bitcast_dynamic-update-slice_fusion.19) | copy-start | bytes 7471108
  124.0 10.7 %collective-permute-start.8 = (f32[19,1,16,256]{3,2,1,0:T(8,128)S(1)}, f32[19,1,16,256]{3,2,1,0:T(8,128)S(1)}, u32[]{:S(2)}, u32[]{:S(2)}) collective-permute-start(f32[19,1,16,256]{3,2,1,0:T(8,128)S(1)} %get-tuple-element.100), channel_id=1, source_target_pairs={{8,0},{16,8},{24,16},{32,24},{40,32},{48,40},{56,48},{64,56},{72,6... | collective-permute-start | bytes 933896 | tf_op jit(solution)/shard_map/ppermute | solution.py:42
  129.9 11.8 %collective-permute-start.9 = (f32[19,1,16,256]{3,2,1,0:T(8,128)S(1)}, f32[19,1,16,256]{3,2,1,0:T(8,128)S(1)}, u32[]{:S(2)}, u32[]{:S(2)}) collective-permute-start(f32[19,1,16,256]{3,2,1,0:T(8,128)S(1)} %get-tuple-element.99), channel_id=1, source_target_pairs={{0,8},{8,16},{16,24},{24,32},{32,40},{40,48},{48,56},{56,64},{64,7... | collective-permute-start | bytes 933896 | tf_op jit(solution)/shard_map/ppermute | solution.py:40
  143.4 41.2 %collective-permute-start.11 = (f32[19,10,1,256]{3,0,2,1:T(8,128)}, f32[19,10,1,256]{3,0,2,1:T(8,128)}, u32[]{:S(2)}, u32[]{:S(2)}) collective-permute-start(f32[19,10,1,256]{3,0,2,1:T(8,128)} %copy.36), channel_id=1, source_target_pairs={{0,1},{1,2},{2,3},{3,4},{4,5},{5,6},{6,7},{8,9},{9,10},{10,11},{11... | collective-permute-start | bytes 583688 | tf_op jit(solution)/shard_map/ppermute | solution.py:40
  145.3 40.6 %collective-permute-start.10 = (f32[19,10,1,256]{3,2,1,0:T(1,128)}, f32[19,10,1,256]{3,2,1,0:T(1,128)}, u32[]{:S(2)}, u32[]{:S(2)}) collective-permute-start(f32[19,10,1,256]{3,2,1,0:T(1,128)} %get-tuple-element.65), channel_id=1, source_target_pairs={{1,0},{2,1},{3,2},{4,3},{5,4},{6,5},{7,6},{9,8},{10,9},{11,10},{12... | collective-permute-start | bytes 583688 | tf_op jit(solution)/shard_map/ppermute | solution.py:42
  153.1 31.1 %copy-start.1 = (f32[19,8,16,256]{3,2,1,0:T(8,128)S(1)}, f32[19,8,16,256]{3,2,1,0:T(8,128)}, u32[]{:S(2)}) copy-start(f32[19,8,16,256]{3,2,1,0:T(8,128)} %copy-done) | copy-start | bytes 7471108
  (34 other events, 146.7 us)
where the time goes:
time: 195 us; the launch traced here: 193 us
  local copies, waits for them, and re-layouts  91.6 us (47%)
  starting transfers between devices  45.3 us (23%)
  other arithmetic  41.4 us (21%)
  waiting for transfers between devices  13.2 us (7%)
    squeeze x38, local copies, waits for them, and re-layouts, adjoint_collide(): pops_list = [populations[index] for index in range(19)]  59.3 us
    ppermute x6, starting transfers between devices, padded(): lax.ppermute(head, axis, [((i + 1) % count, i) for i in range(ends)])  30.2 us
    scatter-add x1, other arithmetic, deliver_seeds(): return empty_field.at[:, target_cell].add(values.T)  15.6 us
    ppermute x6, starting transfers between devices, padded(): lax.ppermute(tail, axis, [(i, (i + 1) % count) for i in range(ends)])  15.1 us
    ppermute x6, waiting for transfers between devices, padded(): lax.ppermute(tail, axis, [(i, (i + 1) % count) for i in range(ends)])  12.1 us
    reshape x1, local copies, waits for them, and re-layouts, body(): seed_field.reshape(channels, width_x, width_y, height)  11.3 us
    unnamed x36, other arithmetic  8.96 us
    convert_element_type x2, local copies, waits for them, and re-layouts, dequantize(): quantized.astype(jnp.float32)  6.38 us
  transfers between devices with their start and end apart: 12, of which 3 were waited for; matrix products, arithmetic and copies ran while one was open for 45% of the time, Pallas kernels for 0%

commit v1 on v0

v1 whole, which is shorter than its diff:
```python
import functools

import jax
import jax.numpy as jnp
from jax import lax
from jax.experimental import pallas as pl
from jax.experimental.pallas import tpu as pltpu
from jax.sharding import PartitionSpec as P

PAIRS = [
    (1, 2, (1, 0, 0)),
    (3, 4, (0, 1, 0)),
    (5, 6, (0, 0, 1)),
    (7, 8, (1, 1, 0)),
    (9, 10, (1, -1, 0)),
    (11, 12, (1, 0, 1)),
    (13, 14, (1, 0, -1)),
    (15, 16, (0, 1, 1)),
    (17, 18, (0, 1, -1)),
]
VEL = [(0, 0, 0)] * 19
for _p, _m, _c in PAIRS:
    VEL[_p] = _c
    VEL[_m] = tuple(-v for v in _c)
OPP = [0] * 19
for _p, _m, _c in PAIRS:
    OPP[_p], OPP[_m] = _m, _p
RELAX = 0.8
F32 = jnp.float32
BX, BY, BZ = 8, 16, 256
EX = 12
LIST = 32


def face_rows(axis, sign):
    near = [i for i in range(19) if VEL[i][axis] in (0, sign)]
    far = [i for i in range(19) if VEL[i][axis] == sign]
    return near, far


vmem = pl.BlockSpec(memory_space=pltpu.VMEM)
anyspace = pl.BlockSpec(memory_space=pl.ANY)


def in_vmem(x):
    return pltpu.with_memory_space_constraint(x, pltpu.VMEM)


def call(body, out_shape, in_specs, args, scratch=(), aliases=None, limit=20 << 20):
    single = not isinstance(out_shape, (tuple, list))
    outs = (out_shape,) if single else tuple(out_shape)
    out_specs = tuple(vmem if isinstance(o, type(pltpu.VMEM((8, 128), F32))) else anyspace for o in outs)
    res = pl.pallas_call(
        body,
        out_shape=outs,
        in_specs=in_specs,
        out_specs=out_specs,
        scratch_shapes=list(scratch),
        input_output_aliases=aliases or {},
        compiler_params=pltpu.CompilerParams(vmem_limit_bytes=limit),
    )(*args)
    return res[0] if single else res


def iota(shape, dim):
    return lax.broadcasted_iota(jnp.int32, shape, dim)


def group_items(values, contact, cell, low, mid, high, pay):
    code = contact[...]
    hot = (iota((16, 128), 0) == code).astype(jnp.bfloat16)
    before = (iota((128, 128), 0) < iota((128, 128), 1)).astype(jnp.bfloat16)
    counts = jnp.dot(hot, before, preferred_element_type=F32)
    rank = jnp.sum(jnp.where(iota((16, 128), 0) == code, counts, 0.0), axis=0, keepdims=True).astype(jnp.int32)
    third = (code >= 3).astype(jnp.int32) + (code >= 6).astype(jnp.int32)
    slot = third * 128 + (code - 3 * third) * LIST + rank
    pay[...] = jnp.zeros((24, 128), F32)
    pay[0:19, :] = values[...]
    pay[19:20, :] = cell[...].astype(F32)
    payload = pay[...]
    for part, out in enumerate((low, mid, high)):
        pick = (iota((128, 128), 0) + 128 * part == slot).astype(F32)
        out[...] = lax.dot_general(
            payload, pick, (((1,), (1,)), ((), ())), precision=lax.Precision.HIGHEST, preferred_element_type=F32
        )


def regroup(left, own, right, down, same, up):
    gx = lax.axis_index("gx")
    a = jnp.where(gx > 0, left[...], 0.0)
    b = own[...]
    c = jnp.where(gx < lax.axis_size("gx") - 1, right[...], 0.0)
    lane = iota((24, 128), 1)
    for j, out in enumerate((down, same, up)):
        ra = pltpu.roll(a, (-LIST * j) % 128, 1)
        rb = pltpu.roll(b, (LIST - LIST * j) % 128, 1)
        rc = pltpu.roll(c, (2 * LIST - LIST * j) % 128, 1)
        out[...] = jnp.where(
            lane < LIST, ra, jnp.where(lane < 2 * LIST, rb, jnp.where(lane < 3 * LIST, rc, 0.0))
        )


def velocities(pops, scale, adj, vel, ext, raw, sems, adj_sem):
    copies = []
    for s in range(2):
        for h in range(2):
            c = pltpu.make_async_copy(
                pops.at[s, :, pl.ds(4 * h, 4)], raw.at[s, :, pl.ds(4 * h, 4)], sems.at[2 * s + h]
            )
            c.start()
            copies.append(c)
    adj_copy = pltpu.make_async_copy(adj, ext.at[:, pl.ds(2, BX)], adj_sem)
    adj_copy.start()
    for s in range(2):
        for h in range(2):
            copies[2 * s + h].wait()

            def plane(x, carry, s=s):
                for b in range(2):
                    table = scale[s, x, pl.ds(b, BY, stride=2), :]

                    def pop(i):
                        f = raw[s, i, x, :, 128 * b : 128 * (b + 1)].astype(F32)
                        return f * jnp.broadcast_to(table[:, i : i + 1], (BY, 128))

                    density = pop(0)
                    mom = [None, None, None]
                    for plus, minus, c in PAIRS:
                        fp, fm = pop(plus), pop(minus)
                        density = density + (fp + fm)
                        d = fp - fm
                        for axis in range(3):
                            if c[axis]:
                                if mom[axis] is None:
                                    mom[axis] = d
                                elif c[axis] > 0:
                                    mom[axis] = mom[axis] + d
                                else:
                                    mom[axis] = mom[axis] - d
                    inv = 1.0 / density
                    for axis in range(3):
                        vel[s, axis, x, :, 128 * b : 128 * (b + 1)] = mom[axis] * inv
                return carry

            lax.fori_loop(4 * h, 4 * h + 4, plane, 0)
    adj_copy.wait()


def scatter(ext_in, vel, solid, down, same, up, ext, to_left, to_right, where_xy, where_z):
    del ext_in
    gy = lax.axis_index("gy")
    high, low = [], []
    for b, ref in enumerate((down, same, up)):
        block = ref[...]
        if b == 0:
            block = jnp.where(gy > 0, block, 0.0)
        elif b == 2:
            block = jnp.where(gy < lax.axis_size("gy") - 1, block, 0.0)
        cell = block[19:20, :].astype(jnp.int32)
        rows, height = cell // BZ, cell % BZ
        mask = (iota((128, 128), 0) == rows).astype(F32).astype(jnp.bfloat16)
        where_xy[:, 128 * b : 128 * (b + 1)] = mask
        hot = (iota((BZ, 128), 0) == height).astype(F32)
        spread = hot.T.astype(jnp.bfloat16)
        where_z[128 * b : 128 * (b + 1), :] = spread
        where_z[384 + 128 * b : 384 + 128 * (b + 1), :] = spread
        hi = block.astype(jnp.bfloat16).astype(F32)
        high.append(hi)
        low.append(block - hi)
    high = jnp.concatenate(high, axis=1)
    low = jnp.concatenate(low, axis=1)
    for i in range(19):
        rows = where_xy[...]
        left = rows * high[i : i + 1, :].astype(jnp.bfloat16)
        right = rows * low[i : i + 1, :].astype(jnp.bfloat16)
        both = jnp.concatenate([left, right], axis=1)
        field = jnp.dot(both, where_z[...], preferred_element_type=F32)
        ext[i, 2 : 2 + BX] = ext[i, 2 : 2 + BX] + field.reshape(BX, BY, BZ)
    for sign, out, near_x, far_x in ((1, to_left, 2, 3), (-1, to_right, 9, 8)):
        near, far = face_rows(0, sign)
        for slot, i in enumerate(near):
            out[slot] = ext[i, near_x]
        for slot, i in enumerate(far):
            out[14 + slot] = ext[i, far_x]
        for axis in range(3):
            out[19 + axis] = vel[1, axis, near_x - 2]
        out[22] = (solid[near_x - 2] > 0).astype(F32)


def y_faces(ext_in, from_left, from_right, vel, solid, ext, to_down, to_up):
    del ext_in
    gx = lax.axis_index("gx")
    inner = gx > 0, gx < lax.axis_size("gx") - 1
    for sign, ref, ok, near_x, far_x in ((-1, from_left, inner[0], 1, 0), (1, from_right, inner[1], 10, 11)):
        near, far = face_rows(0, sign)
        for slot, i in enumerate(near):
            ext[i, near_x] = jnp.where(ok, ref[slot], 0.0)
        for slot, i in enumerate(far):
            ext[i, far_x] = jnp.where(ok, ref[14 + slot], 0.0)
    for sign, out, near_y, far_y in ((1, to_down, 0, 1), (-1, to_up, BY - 1, BY - 2)):
        near, far = face_rows(1, sign)
        out[...] = jnp.zeros((23, 16, BZ), F32)
        for base, pops, y in ((0, near, near_y), (14, far, far_y)):
            for slot, i in enumerate(pops):
                for x in range(EX):
                    if needed(i, x):
                        out[base + slot, x : x + 1, :] = ext[i, x, y : y + 1, :]
        for axis in range(3):
            out[19 + axis, 1:2, :] = from_left[19 + axis, near_y : near_y + 1, :]
            out[19 + axis, 10:11, :] = from_right[19 + axis, near_y : near_y + 1, :]
            for x in range(BX):
                out[19 + axis, x + 2 : x + 3, :] = vel[1, axis, x, near_y : near_y + 1, :]
        out[22, 1:2, :] = from_left[22, near_y : near_y + 1, :]
        out[22, 10:11, :] = from_right[22, near_y : near_y + 1, :]
        for x in range(BX):
            out[22, x + 2 : x + 3, :] = (solid[x, near_y : near_y + 1, :] > 0).astype(F32)


def needed(i, x):
    if x == 0:
        return VEL[i][0] == -1
    if x == 1:
        return VEL[i][0] in (0, -1)
    if x == EX - 2:
        return VEL[i][0] in (0, 1)
    if x == EX - 1:
        return VEL[i][0] == 1
    return True


def adjoint_collide(u, is_solid, r, want):
    square = u[0] * u[0] + u[1] * u[1] + u[2] * u[2]
    axis_sum = diag_sum = axis_quad = diag_quad = None
    axis_mom = [None, None, None]
    diag_mom = [None, None, None]

    def plus(a, b):
        return b if a is None else a + b

    for n, (ip, im, c) in enumerate(PAIRS):
        s, d = r[ip] + r[im], r[ip] - r[im]
        p = None
        for axis in range(3):
            if c[axis]:
                p = u[axis] if p is None else (p + u[axis] if c[axis] > 0 else p - u[axis])
        q = p * s
        m = d + 3.0 * q
        if n < 3:
            axis_sum, axis_quad = plus(axis_sum, s), plus(axis_quad, q * p)
            axis_mom[n] = m
        else:
            diag_sum, diag_quad = plus(diag_sum, s), plus(diag_quad, q * p)
            for axis in range(3):
                if c[axis] > 0:
                    diag_mom[axis] = plus(diag_mom[axis], m)
                elif c[axis] < 0:
                    diag_mom[axis] = diag_mom[axis] - m
    scale = 1.0 / RELAX
    keep = 1.0 - scale
    total = (scale / 3.0) * r[0] + (scale / 18.0) * axis_sum + (scale / 36.0) * diag_sum
    quad = (4.5 * scale / 18.0) * axis_quad + (4.5 * scale / 36.0) * diag_quad
    density = total * (1.0 + 1.5 * square) - quad
    triple = 3.0 * total
    grad = [
        (3.0 * scale / 18.0) * axis_mom[a] + (3.0 * scale / 36.0) * diag_mom[a] - triple * u[a] for a in range(3)
    ]
    out = {}
    if 0 in want:
        out[0] = jnp.where(is_solid, r[0], keep * r[0] + density)
    for ip, im, c in PAIRS:
        if ip not in want and im not in want:
            continue
        g = None
        for axis in range(3):
            if c[axis]:
                g = grad[axis] if g is None else (g + grad[axis] if c[axis] > 0 else g - grad[axis])
        if ip in want:
            out[ip] = jnp.where(is_solid, r[im], keep * r[ip] + (density + g))
        if im in want:
            out[im] = jnp.where(is_solid, r[ip], keep * r[im] + (density - g))
    return out


def shift_z(v, step):
    if step == 0:
        return v
    lane = iota(v.shape, 1)
    if step > 0:
        return jnp.where(lane == BZ - 1, 0.0, pltpu.roll(v, BZ - 1, 1))
    return jnp.where(lane == 0, 0.0, pltpu.roll(v, 1, 1))


NEAR_DOWN = {i: n for n, i in enumerate(face_rows(1, -1)[0])}
NEAR_UP = {i: n for n, i in enumerate(face_rows(1, 1)[0])}
FAR_DOWN = {i: n for n, i in enumerate(face_rows(1, -1)[1])}
FAR_UP = {i: n for n, i in enumerate(face_rows(1, 1)[1])}
ALL = list(range(19))


def read_plane(field, low_face, high_face, x, i, low_slot, high_slot):
    cx, cy, cz = VEL[i]
    v = field[i, x + cx]
    if cy:
        row = iota(v.shape, 0)
        if cy > 0:
            edge = high_face[high_slot[i], pl.ds(x + cx, 1), :]
            v = jnp.where(row == BY - 1, jnp.broadcast_to(edge, v.shape), pltpu.roll(v, BY - 1, 0))
        else:
            edge = low_face[low_slot[i], pl.ds(x + cx, 1), :]
            v = jnp.where(row == 0, jnp.broadcast_to(edge, v.shape), pltpu.roll(v, 1, 0))
    return shift_z(v, cz)


def collide_block(reads, load_u, load_solid, want, store):
    for h in range(2):
        for b in range(2):
            rows, lanes = slice(8 * h, 8 * h + 8), slice(128 * b, 128 * b + 128)
            r = [reads[i, rows, lanes] for i in range(19)]
            u = [load_u(axis, rows, lanes) for axis in range(3)]
            out = adjoint_collide(u, load_solid(rows, lanes), r, want)
            for i in want:
                store(i, rows, lanes, out[i])


def two_steps(
    ext, from_left, from_right, from_down, from_up, to_down, to_up, vel, solid,
    initial, middle, mid_ext, first, low_near, high_near, low_face, high_face, reads, mid_sems, first_sems,
):
    gx, gy = lax.axis_index("gx"), lax.axis_index("gy")
    in_left, in_right = gx > 0, gx < lax.axis_size("gx") - 1
    in_down, in_up = gy > 0, gy < lax.axis_size("gy") - 1
    for n in range(14):
        low_near[n] = jnp.where(in_down, from_down[n], 0.0)
        high_near[n] = jnp.where(in_up, from_up[n], 0.0)

    for x, ref, ok, sign in ((1, from_left, in_left, -1), (EX - 2, from_right, in_right, 1)):
        for i in range(19):
            reads[i] = read_plane(ext, low_near, high_near, x, i, NEAR_DOWN, NEAR_UP)

        def keep(i, rows, lanes, value, x=x, ok=ok):
            mid_ext[i, x, rows, lanes] = jnp.where(ok, value, 0.0)

        collide_block(
            reads,
            lambda axis, rows, lanes, ref=ref: ref[19 + axis, rows, lanes],
            lambda rows, lanes, ref=ref: ref[22, rows, lanes] > 0.0,
            face_rows(0, sign)[1],
            keep,
        )

    for ref, mine, near, far, sign, ok, out in (
        (from_down, to_down, NEAR_DOWN, FAR_DOWN, -1, in_down, low_face),
        (from_up, to_up, NEAR_UP, FAR_UP, 1, in_up, high_face),
    ):
        mine_near = NEAR_UP if sign < 0 else NEAR_DOWN
        for i in range(19):
            cx, cy, cz = VEL[i]
            if cy == 0:
                v = ref[near[i]]
            elif cy == sign:
                v = ref[14 + far[i]]
            else:
                v = mine[mine_near[i]]
            if cx:
                v = pltpu.roll(v, (-cx) % 16, 0)
            reads[i] = shift_z(v, cz)
        row = iota((8, 128), 0)

        def keep_row(i, rows, lanes, value, out=out, far=far, ok=ok):
            x = row + rows.start
            good = ok & ((x > 1) | in_left) & ((x < EX - 2) | in_right)
            out[far[i], rows, lanes] = jnp.where(good, value, 0.0)

        collide_block(
            reads,
            lambda axis, rows, lanes, ref=ref: ref[19 + axis, rows, lanes],
            lambda rows, lanes, ref=ref: ref[22, rows, lanes] > 0.0,
            face_rows(1, sign)[1],
            keep_row,
        )

    def mid_copy(x):
        return pltpu.make_async_copy(mid_ext.at[:, pl.ds(x + 2, 1)], middle.at[:, pl.ds(x, 1)], mid_sems.at[x])

    def first_copy(x):
        return pltpu.make_async_copy(first.at[:, pl.ds(x, 1)], initial.at[:, pl.ds(x, 1)], first_sems.at[x])

    def mid_plane(x, carry):
        for i in range(19):
            reads[i] = read_plane(ext, low_near, high_near, x + 2, i, NEAR_DOWN, NEAR_UP)

        def keep(i, rows, lanes, value):
            mid_ext[i, x + 2, rows, lanes] = value

        collide_block(
            reads,
            lambda axis, rows, lanes: vel[1, axis, x, rows, lanes],
            lambda rows, lanes: solid[x, rows, lanes] > 0,
            ALL,
            keep,
        )
        mid_copy(x).start()
        return carry

    lax.fori_loop(0, BX, mid_plane, 0)

    def first_plane(x, carry):
        for i in range(19):
            reads[i] = read_plane(mid_ext, low_face, high_face, x + 2, i, FAR_DOWN, FAR_UP)

        def keep(i, rows, lanes, value):
            first[i, x, rows, lanes] = value

        collide_block(
            reads,
            lambda axis, rows, lanes: vel[0, axis, x, rows, lanes],
            lambda rows, lanes: solid[x, rows, lanes] > 0,
            ALL,
            keep,
        )
        first_copy(x).start()
        return carry

    lax.fori_loop(0, BX, first_plane, 0)

    def finish(x, carry):
        mid_copy(x).wait()
        first_copy(x).wait()
        return carry

    lax.fori_loop(0, BX, finish, 0)


def shifted(value, axis, step):
    count = lax.axis_size(axis)
    return lax.ppermute(value, axis, [(i, (i + step) % count) for i in range(count)])


def body(adj_later, saved_pops, saved_scale, solid, seed_values, seed_contact, seed_cell):
    block = pltpu.VMEM((24, 128), F32)
    low, mid, high = call(
        group_items,
        (block,) * 3,
        [vmem] * 3,
        (seed_values.T, seed_contact.reshape(1, 128), seed_cell.reshape(1, 128)),
        scratch=[pltpu.VMEM((24, 128), F32)],
    )
    left = shifted(high, "gx", 1)
    right = shifted(low, "gx", -1)

    scale = saved_scale.transpose(0, 2, 3, 4, 1).reshape(2, BX, 2 * BY, 19)
    vel, ext = call(
        velocities,
        (pltpu.VMEM((2, 3, BX, BY, BZ), F32), pltpu.VMEM((19, EX, BY, BZ), F32)),
        [anyspace, vmem, anyspace],
        (saved_pops, scale, adj_later),
        scratch=[
            pltpu.VMEM((2, 19, BX, BY, BZ), jnp.bfloat16),
            pltpu.SemaphoreType.DMA((4,)),
            pltpu.SemaphoreType.DMA(()),
        ],
    )

    down, same, up = call(regroup, (block,) * 3, [vmem] * 3, (in_vmem(left), mid, in_vmem(right)))
    from_low = shifted(up, "gy", 1)
    from_high = shifted(down, "gy", -1)

    solid_v = in_vmem(solid)
    face = pltpu.VMEM((23, BY, BZ), F32)
    ext, to_left, to_right = call(
        scatter,
        (pltpu.VMEM((19, EX, BY, BZ), F32), face, face),
        [vmem] * 6,
        (ext, vel, solid_v, in_vmem(from_low), same, in_vmem(from_high)),
        scratch=[pltpu.VMEM((128, 384), jnp.bfloat16), pltpu.VMEM((768, BZ), jnp.bfloat16)],
        aliases={0: 0},
    )
    from_left = in_vmem(shifted(to_right, "gx", 1))
    from_right = in_vmem(shifted(to_left, "gx", -1))
    row_face = pltpu.VMEM((23, 16, BZ), F32)
    ext, to_down, to_up = call(
        y_faces,
        (pltpu.VMEM((19, EX, BY, BZ), F32), row_face, row_face),
        [vmem] * 5,
        (ext, from_left, from_right, vel, solid_v),
        aliases={0: 0},
    )
    from_down = in_vmem(shifted(to_up, "gy", 1))
    from_up = in_vmem(shifted(to_down, "gy", -1))
    field = jax.ShapeDtypeStruct((19, BX, BY, BZ), F32)
    return call(
        two_steps,
        (field, field),
        [vmem] * 9,
        (ext, from_left, from_right, from_down, from_up, to_down, to_up, vel, solid_v),
        scratch=[
            pltpu.VMEM((19, EX, BY, BZ), F32),
            pltpu.VMEM((19, BX, BY, BZ), F32),
            pltpu.VMEM((14, 16, BZ), F32),
            pltpu.VMEM((14, 16, BZ), F32),
            pltpu.VMEM((5, 16, BZ), F32),
            pltpu.VMEM((5, 16, BZ), F32),
            pltpu.VMEM((19, BY, BZ), F32),
            pltpu.SemaphoreType.DMA((BX,)),
            pltpu.SemaphoreType.DMA((BX,)),
        ],
    )


def solution(mesh):
    return jax.shard_map(
        body,
        mesh=mesh,
        in_specs=(
            P(None, "gx", "gy", None),
            P(None, None, "gx", "gy", None),
            P(None, None, "gx", "gy", None),
            P("gx", "gy", None),
            P(("gx", "gy"), None),
            P(("gx", "gy"), None),
            P(("gx", "gy")),
        ),
        out_specs=(P(None, "gx", "gy", None), P(None, "gx", "gy", None)),
        check_vma=False,
    )
```

time: 195 us -> 52.8 us (0.27)
  the two profiles are of different devices: /device:TPU:24 before, /device:TPU:6 now
where the time goes in v1:
time: 52.8 us; the launch traced here: 52.6 us
  starting transfers between devices  19.1 us (36%)
  waiting for transfers between devices  16.4 us (31%)
  Pallas kernels  9.99 us (19%)
  local copies, waits for them, and re-layouts  6.37 us (12%)
  between operations  0.71 us (1%)
    ppermute x8, starting transfers between devices, shifted(): lax.ppermute(value, axis, [(i, (i + step) % count) for i in range(count)])  19.1 us
    ppermute x8, waiting for transfers between devices, shifted(): lax.ppermute(value, axis, [(i, (i + step) % count) for i in range(count)])  16.4 us
    pallas_call x6, Pallas kernels, call(): pl.pallas_call(body, out_shape=outs, in_specs=in_specs, out_specs=out_spe...  9.99 us
    unnamed x14, local copies, waits for them, and re-layouts  6.37 us
  transfers between devices with their start and end apart: 8, of which 5 were waited for; matrix products, arithmetic and copies ran while one was open for 0% of the time, Pallas kernels for 7%

profile of v1, /device:TPU:6, one launch (start us, length us, event | category | flops | bytes accessed | tf_op | source)
XLA Modules:
  0.0 52.6 jit_solution(16794234694732755895)
XLA Ops:
  0.6 0.7 %copy-done.4 = f32[128,19]{0,1:T(8,128)S(1)} copy-done((f32[128,19]{0,1:T(8,128)S(1)}, f32[128,19]{0,1:T(8,128)}, u32[]{:S(2)}) %copy-start.4) | copy-done | bytes 9752
  1.3 0.7 %copy-done.5 = s32[128,1]{0,1:T(1,128)S(1)} copy-done((s32[128,1]{0,1:T(1,128)S(1)}, s32[128,1]{0,1:T(1,128)}, u32[]{:S(2)}) %copy-start.5) | copy-done | bytes 536
  2.0 0.7 %copy-done.6 = s32[128]{0:T(128)S(1)} copy-done((s32[128]{0:T(128)S(1)}, s32[128]{0:T(128)}, u32[]{:S(2)}) %copy-start.6) | copy-done | bytes 536
  2.6 0.5 %shard_map.87 = (f32[24,128]{1,0:T(8,128)S(1)}, f32[24,128]{1,0:T(8,128)S(1)}, f32[24,128]{1,0:T(8,128)S(1)}) custom-call(f32[19,128]{1,0:T(8,128)S(1)} %bitcast.7, s32[1,128]{1,0:T(1,128)S(1)} %bitcast.8, s32[1,128]{1,0:T(1,128)S(1)} %bitcast.9), custom_call_target="tpu_custom_call" | custom-call | tf_op jit(solution)/shard_map/pallas_call | solution.py:53
  3.2 0.0 collective-permute-start
  3.2 8.0 %collective-permute-start.1 = (f32[24,128]{1,0:T(8,128)S(1)}, f32[24,128]{1,0:T(8,128)S(1)}, u32[]{:S(2)}, u32[]{:S(2)}) collective-permute-start(f32[24,128]{1,0:T(8,128)S(1)} %get-tuple-element.20), channel_id=1, source_target_pairs={{0,248},{8,0},{16,8},{24,16},{32,24},{40,32},{48,40},{56,48},{64,5... | collective-permute-start | bytes 36872 | tf_op jit(solution)/shard_map/ppermute | solution.py:436
  11.2 1.3 %collective-permute-done.left = f32[24,128]{1,0:T(8,128)S(1)} collective-permute-done((f32[24,128]{1,0:T(8,128)S(1)}, f32[24,128]{1,0:T(8,128)S(1)}, u32[]{:S(2)}, u32[]{:S(2)}) %collective-permute-start) | collective-permute-done | bytes 12320 | tf_op jit(solution)/shard_map/ppermute | solution.py:436
  12.5 0.1 collective-permute-done.1.right
  12.6 0.1 shard_map.88
  12.7 0.7 %collective-permute-start.2 = (f32[24,128]{1,0:T(8,128)S(1)}, f32[24,128]{1,0:T(8,128)S(1)}, u32[]{:S(2)}, u32[]{:S(2)}) collective-permute-start(f32[24,128]{1,0:T(8,128)S(1)} %get-tuple-element.21), channel_id=1, source_target_pairs={{0,1},{1,2},{2,3},{3,4},{4,5},{5,6},{6,7},{7,0},{8,9},{9,10},{10,1... | collective-permute-start | bytes 36872 | tf_op jit(solution)/shard_map/ppermute | solution.py:436
  13.4 1.4 %collective-permute-start.3 = (f32[24,128]{1,0:T(8,128)S(1)}, f32[24,128]{1,0:T(8,128)S(1)}, u32[]{:S(2)}, u32[]{:S(2)}) collective-permute-start(f32[24,128]{1,0:T(8,128)S(1)} %get-tuple-element.23), channel_id=1, source_target_pairs={{0,7},{1,0},{2,1},{3,2},{4,3},{5,4},{6,5},{7,6},{8,15},{9,8},{10,9... | collective-permute-start | bytes 36872 | tf_op jit(solution)/shard_map/ppermute | solution.py:436
  14.8 1.7 %copy-done = bf16[2,19,8,16,256]{4,3,2,1,0:T(8,128)(2,1)S(1)} copy-done((bf16[2,19,8,16,256]{4,3,2,1,0:T(8,128)(2,1)S(1)}, bf16[2,19,8,16,256]{4,3,2,1,0:T(8,128)(2,1)}, u32[]{:S(2)}) %copy-start) | copy-done | bytes 2490392
  16.5 1.7 %copy-done.1 = f32[19,8,16,256]{3,2,1,0:T(8,128)S(1)} copy-done((f32[19,8,16,256]{3,2,1,0:T(8,128)S(1)}, f32[19,8,16,256]{3,2,1,0:T(8,128)}, u32[]{:S(2)}) %copy-start.1) | copy-done | bytes 2490392
  18.2 0.9 %copy-done.3 = f32[2,19,8,16,2]{1,4,3,2,0:T(2,128)S(1)} copy-done((f32[2,19,8,16,2]{1,4,3,2,0:T(2,128)S(1)}, f32[2,19,8,16,2]{1,4,3,2,0:T(2,128)}, u32[]{:S(2)}) %copy-start.3) | copy-done | bytes 38936
  19.1 3.6 %shard_map.86 = (f32[2,3,8,16,256]{4,3,2,1,0:T(8,128)S(1)}, f32[19,12,16,256]{3,2,1,0:T(8,128)S(1)}) custom-call(bf16[2,19,8,16,256]{4,3,2,1,0:T(8,128)(2,1)S(1)} %copy-done, f32[2,8,32,19]{3,2,1,0:T(8,128)S(1)} %bitcast.6, f32[19,8,16,256]{3,2,1,0:T(8,128)S(1)} %copy-done.1), custom_call_target="tpu_custom_call" | custom-call | tf_op jit(solution)/shard_map/pallas_call | solution.py:53
  22.8 1.3 %shard_map.89 = (f32[19,12,16,256]{3,2,1,0:T(8,128)S(1)}, f32[23,16,256]{2,1,0:T(8,128)S(1)}, f32[23,16,256]{2,1,0:T(8,128)S(1)}) custom-call(f32[19,12,16,256]{3,2,1,0:T(8,128)S(1)} %get-tuple-element.16.ext_in, f32[2,3,8,16,256]{4,3,2,1,0:T(8,128)S(1)} %get-tuple-element.17.vel, s32[8,16,256]{2,1,0:T(8,128)S(1)} %copy-done.2, ...), custom_call_target="tpu_custom_call", output_to_operand_aliasing={{0}: (0, {})} | custom-call | tf_op jit(solution)/shard_map/pallas_call | solution.py:53
  24.1 0.1 collective-permute-start.4
  24.2 5.3 %collective-permute-start.5 = (f32[23,16,256]{2,1,0:T(8,128)S(1)}, f32[23,16,256]{2,1,0:T(8,128)S(1)}, u32[]{:S(2)}, u32[]{:S(2)}) collective-permute-start(f32[23,16,256]{2,1,0:T(8,128)S(1)} %get-tuple-element.26), channel_id=1, source_target_pairs={{0,248},{8,0},{16,8},{24,16},{32,24},{40,32},{48,40},{56,48},{64,5... | collective-permute-start | bytes 1130504 | tf_op jit(solution)/shard_map/ppermute | solution.py:436
  29.5 5.3 %collective-permute-done.4.from_left = f32[23,16,256]{2,1,0:T(8,128)S(1)} collective-permute-done((f32[23,16,256]{2,1,0:T(8,128)S(1)}, f32[23,16,256]{2,1,0:T(8,128)S(1)}, u32[]{:S(2)}, u32[]{:S(2)}) %collective-permute-start.4) | collective-permute-done | bytes 376864 | tf_op jit(solution)/shard_map/ppermute | solution.py:436
  34.8 0.3 shard_map.90
  35.1 3.6 %collective-permute-start.6 = (f32[23,16,256]{2,1,0:T(8,128)S(1)}, f32[23,16,256]{2,1,0:T(8,128)S(1)}, u32[]{:S(2)}, u32[]{:S(2)}) collective-permute-start(f32[23,16,256]{2,1,0:T(8,128)S(1)} %get-tuple-element.28.to_up), channel_id=1, source_target_pairs={{0,1},{1,2},{2,3},{3,4},{4,5},{5,6},{6,7},{7,0},{8,9},{9,10},{10,1... | collective-permute-start | bytes 1130504 | tf_op jit(solution)/shard_map/ppermute | solution.py:436
  38.7 5.1 %collective-permute-done.6.from_down = f32[23,16,256]{2,1,0:T(8,128)S(1)} collective-permute-done((f32[23,16,256]{2,1,0:T(8,128)S(1)}, f32[23,16,256]{2,1,0:T(8,128)S(1)}, u32[]{:S(2)}, u32[]{:S(2)}) %collective-permute-start.6) | collective-permute-done | bytes 376864 | tf_op jit(solution)/shard_map/ppermute | solution.py:436
  43.8 4.6 %collective-permute-done.7.from_up = f32[23,16,256]{2,1,0:T(8,128)S(1)} collective-permute-done((f32[23,16,256]{2,1,0:T(8,128)S(1)}, f32[23,16,256]{2,1,0:T(8,128)S(1)}, u32[]{:S(2)}, u32[]{:S(2)}) %collective-permute-start.7) | collective-permute-done | bytes 376864 | tf_op jit(solution)/shard_map/ppermute | solution.py:436
  48.4 4.2 %shard_map.91 = (f32[19,8,16,256]{3,2,1,0:T(8,128)}, f32[19,8,16,256]{3,2,1,0:T(8,128)}) custom-call(f32[19,12,16,256]{3,2,1,0:T(8,128)S(1)} %get-tuple-element.27.ext, f32[23,16,256]{2,1,0:T(8,128)S(1)} %collective-permute-done.4.from_left, f32[23,16,256]{2,1,0:T(8,128)S(1)} %collective-permute-done.5.from_right, ...), custom_call_target="tpu_custom_call" | custom-call | tf_op jit(solution)/shard_map/pallas_call | solution.py:53
  (12 shorter events, 0.0 us)
Async XLA Ops:
  0.6 0.7 %copy-start.4 = (f32[128,19]{0,1:T(8,128)S(1)}, f32[128,19]{0,1:T(8,128)}, u32[]{:S(2)}) copy-start(f32[128,19]{0,1:T(8,128)} %param.11) | copy-start | bytes 29188
  1.3 0.7 %copy-start.5 = (s32[128,1]{0,1:T(1,128)S(1)}, s32[128,1]{0,1:T(1,128)}, u32[]{:S(2)}) copy-start(s32[128,1]{0,1:T(1,128)} %param.12) | copy-start | bytes 1540
  2.0 0.7 %copy-start.6 = (s32[128]{0:T(128)S(1)}, s32[128]{0:T(128)}, u32[]{:S(2)}) copy-start(s32[128]{0:T(128)} %param.13) | copy-start | bytes 1540
  3.2 9.3 %collective-permute-start = (f32[24,128]{1,0:T(8,128)S(1)}, f32[24,128]{1,0:T(8,128)S(1)}, u32[]{:S(2)}, u32[]{:S(2)}) collective-permute-start(f32[24,128]{1,0:T(8,128)S(1)} %get-tuple-element.18), channel_id=1, source_target_pairs={{0,8},{8,16},{16,24},{24,32},{32,40},{40,48},{48,56},{56,64},{64,7... | collective-permute-start | bytes 36872 | tf_op jit(solution)/shard_map/ppermute | solution.py:436
  3.2 9.4 %collective-permute-start.1 = (f32[24,128]{1,0:T(8,128)S(1)}, f32[24,128]{1,0:T(8,128)S(1)}, u32[]{:S(2)}, u32[]{:S(2)}) collective-permute-start(f32[24,128]{1,0:T(8,128)S(1)} %get-tuple-element.20), channel_id=1, source_target_pairs={{0,248},{8,0},{16,8},{24,16},{32,24},{40,32},{48,40},{56,48},{64,5... | collective-permute-start | bytes 36872 | tf_op jit(solution)/shard_map/ppermute | solution.py:436
  12.7 10.1 %collective-permute-start.2 = (f32[24,128]{1,0:T(8,128)S(1)}, f32[24,128]{1,0:T(8,128)S(1)}, u32[]{:S(2)}, u32[]{:S(2)}) collective-permute-start(f32[24,128]{1,0:T(8,128)S(1)} %get-tuple-element.21), channel_id=1, source_target_pairs={{0,1},{1,2},{2,3},{3,4},{4,5},{5,6},{6,7},{7,0},{8,9},{9,10},{10,1... | collective-permute-start | bytes 36872 | tf_op jit(solution)/shard_map/ppermute | solution.py:436
  13.4 9.4 %collective-permute-start.3 = (f32[24,128]{1,0:T(8,128)S(1)}, f32[24,128]{1,0:T(8,128)S(1)}, u32[]{:S(2)}, u32[]{:S(2)}) collective-permute-start(f32[24,128]{1,0:T(8,128)S(1)} %get-tuple-element.23), channel_id=1, source_target_pairs={{0,7},{1,0},{2,1},{3,2},{4,3},{5,4},{6,5},{7,6},{8,15},{9,8},{10,9... | collective-permute-start | bytes 36872 | tf_op jit(solution)/shard_map/ppermute | solution.py:436
  14.8 1.7 %copy-start = (bf16[2,19,8,16,256]{4,3,2,1,0:T(8,128)(2,1)S(1)}, bf16[2,19,8,16,256]{4,3,2,1,0:T(8,128)(2,1)}, u32[]{:S(2)}) copy-start(bf16[2,19,8,16,256]{4,3,2,1,0:T(8,128)(2,1)} %pops.1) | copy-start | bytes 7471108
  16.5 1.7 %copy-start.1 = (f32[19,8,16,256]{3,2,1,0:T(8,128)S(1)}, f32[19,8,16,256]{3,2,1,0:T(8,128)}, u32[]{:S(2)}) copy-start(f32[19,8,16,256]{3,2,1,0:T(8,128)} %adj.1) | copy-start | bytes 7471108
  18.2 0.9 %copy-start.3 = (f32[2,19,8,16,2]{1,4,3,2,0:T(2,128)S(1)}, f32[2,19,8,16,2]{1,4,3,2,0:T(2,128)}, u32[]{:S(2)}) copy-start(f32[2,19,8,16,2]{1,4,3,2,0:T(2,128)} %param.9) | copy-start | bytes 116740
  19.1 3.7 %copy-start.2 = (s32[8,16,256]{2,1,0:T(8,128)S(1)}, s32[8,16,256]{2,1,0:T(8,128)}, u32[]{:S(2)}) copy-start(s32[8,16,256]{2,1,0:T(8,128)} %solid.5) | copy-start | bytes 393220
  24.1 10.7 %collective-permute-start.4 = (f32[23,16,256]{2,1,0:T(8,128)S(1)}, f32[23,16,256]{2,1,0:T(8,128)S(1)}, u32[]{:S(2)}, u32[]{:S(2)}) collective-permute-start(f32[23,16,256]{2,1,0:T(8,128)S(1)} %get-tuple-element.25), channel_id=1, source_target_pairs={{0,8},{8,16},{16,24},{24,32},{32,40},{40,48},{48,56},{56,64},{64,7... | collective-permute-start | bytes 1130504 | tf_op jit(solution)/shard_map/ppermute | solution.py:436
  24.2 10.6 %collective-permute-start.5 = (f32[23,16,256]{2,1,0:T(8,128)S(1)}, f32[23,16,256]{2,1,0:T(8,128)S(1)}, u32[]{:S(2)}, u32[]{:S(2)}) collective-permute-start(f32[23,16,256]{2,1,0:T(8,128)S(1)} %get-tuple-element.26), channel_id=1, source_target_pairs={{0,248},{8,0},{16,8},{24,16},{32,24},{40,32},{48,40},{56,48},{64,5... | collective-permute-start | bytes 1130504 | tf_op jit(solution)/shard_map/ppermute | solution.py:436
  35.1 8.7 %collective-permute-start.6 = (f32[23,16,256]{2,1,0:T(8,128)S(1)}, f32[23,16,256]{2,1,0:T(8,128)S(1)}, u32[]{:S(2)}, u32[]{:S(2)}) collective-permute-start(f32[23,16,256]{2,1,0:T(8,128)S(1)} %get-tuple-element.28.to_up), channel_id=1, source_target_pairs={{0,1},{1,2},{2,3},{3,4},{4,5},{5,6},{6,7},{7,0},{8,9},{9,10},{10,1... | collective-permute-start | bytes 1130504 | tf_op jit(solution)/shard_map/ppermute | solution.py:436
  38.7 9.7 %collective-permute-start.7 = (f32[23,16,256]{2,1,0:T(8,128)S(1)}, f32[23,16,256]{2,1,0:T(8,128)S(1)}, u32[]{:S(2)}, u32[]{:S(2)}) collective-permute-start(f32[23,16,256]{2,1,0:T(8,128)S(1)} %get-tuple-element.29.to_down), channel_id=1, source_target_pairs={{0,7},{1,0},{2,1},{3,2},{4,3},{5,4},{6,5},{7,6},{8,15},{9,8},{10,9... | collective-permute-start | bytes 1130504 | tf_op jit(solution)/shard_map/ppermute | solution.py:436

commit v2 on v1

v2 whole, which is shorter than its diff:
```python
import functools

import jax
import jax.numpy as jnp
from jax import lax
from jax.experimental import pallas as pl
from jax.experimental.pallas import tpu as pltpu
from jax.sharding import PartitionSpec as P

PAIRS = [
    (1, 2, (1, 0, 0)),
    (3, 4, (0, 1, 0)),
    (5, 6, (0, 0, 1)),
    (7, 8, (1, 1, 0)),
    (9, 10, (1, -1, 0)),
    (11, 12, (1, 0, 1)),
    (13, 14, (1, 0, -1)),
    (15, 16, (0, 1, 1)),
    (17, 18, (0, 1, -1)),
]
VEL = [(0, 0, 0)] * 19
for _p, _m, _c in PAIRS:
    VEL[_p] = _c
    VEL[_m] = tuple(-v for v in _c)
OPP = [0] * 19
for _p, _m, _c in PAIRS:
    OPP[_p], OPP[_m] = _m, _p
RELAX = 0.8
F32 = jnp.float32
BX, BY, BZ = 8, 16, 256
EX = 12
LIST = 32


def face_rows(axis, sign):
    near = [i for i in range(19) if VEL[i][axis] in (0, sign)]
    far = [i for i in range(19) if VEL[i][axis] == sign]
    return near, far


vmem = pl.BlockSpec(memory_space=pltpu.VMEM)
anyspace = pl.BlockSpec(memory_space=pl.ANY)


hbm = pl.BlockSpec(memory_space=pltpu.HBM)


def in_vmem(x):
    return pltpu.with_memory_space_constraint(x, pltpu.VMEM)


def in_hbm(x):
    return pltpu.with_memory_space_constraint(x, pltpu.HBM)


def call(body, out_shape, in_specs, args, scratch=(), aliases=None, limit=20 << 20):
    single = not isinstance(out_shape, (tuple, list))
    outs = (out_shape,) if single else tuple(out_shape)
    out_specs = tuple(vmem if isinstance(o, type(pltpu.VMEM((8, 128), F32))) else anyspace for o in outs)
    res = pl.pallas_call(
        body,
        out_shape=outs,
        in_specs=in_specs,
        out_specs=out_specs,
        scratch_shapes=list(scratch),
        input_output_aliases=aliases or {},
        compiler_params=pltpu.CompilerParams(vmem_limit_bytes=limit),
    )(*args)
    return res[0] if single else res


def iota(shape, dim):
    return lax.broadcasted_iota(jnp.int32, shape, dim)


NEAR_DOWN = {i: n for n, i in enumerate(face_rows(1, -1)[0])}
NEAR_UP = {i: n for n, i in enumerate(face_rows(1, 1)[0])}
FAR_DOWN = {i: n for n, i in enumerate(face_rows(1, -1)[1])}
FAR_UP = {i: n for n, i in enumerate(face_rows(1, 1)[1])}
ALL = list(range(19))


def plane_velocity(pop, store):
    density = pop(0)
    mom = [None, None, None]
    for plus, minus, c in PAIRS:
        fp, fm = pop(plus), pop(minus)
        density = density + (fp + fm)
        d = fp - fm
        for axis in range(3):
            if c[axis]:
                if mom[axis] is None:
                    mom[axis] = d
                elif c[axis] > 0:
                    mom[axis] = mom[axis] + d
                else:
                    mom[axis] = mom[axis] - d
    inv = 1.0 / density
    for axis in range(3):
        store(axis, mom[axis] * inv)


def group_items(values, contact, cell, low, mid, high, pay, own_values, own_contact, own_cell, sems):
    copies = [
        pltpu.make_async_copy(src, dst, sems.at[n])
        for n, (src, dst) in enumerate(((contact, own_contact), (cell, own_cell), (values, own_values)))
    ]
    for c in copies:
        c.start()
    for c in copies:
        c.wait()
    code = own_contact[...]
    hot = (iota((16, 128), 0) == code).astype(jnp.bfloat16)
    before = (iota((128, 128), 0) < iota((128, 128), 1)).astype(jnp.bfloat16)
    counts = jnp.dot(hot, before, preferred_element_type=F32)
    rank = jnp.sum(jnp.where(iota((16, 128), 0) == code, counts, 0.0), axis=0, keepdims=True).astype(jnp.int32)
    third = (code >= 3).astype(jnp.int32) + (code >= 6).astype(jnp.int32)
    slot = third * 128 + (code - 3 * third) * LIST + rank
    pay[...] = jnp.zeros((24, 128), F32)
    pay[0:19, :] = own_values[...]
    pay[19:20, :] = own_cell[...].astype(F32)
    payload = pay[...]
    for part, out in enumerate((low, mid, high)):
        pick = (iota((128, 128), 0) + 128 * part == slot).astype(F32)
        out[...] = lax.dot_general(
            payload, pick, (((1,), (1,)), ((), ())), precision=lax.Precision.HIGHEST, preferred_element_type=F32
        )


def velocity_planes(pops, scale, step, vel, raw, table_all, sems):
    scale_copy = pltpu.make_async_copy(scale.at[step], table_all, sems.at[0])
    scale_copy.start()
    copies = []
    for h in range(2):
        c = pltpu.make_async_copy(pops.at[step, :, pl.ds(4 * h, 4)], raw.at[:, pl.ds(4 * h, 4)], sems.at[1 + h])
        c.start()
        copies.append(c)
    yield
    scale_copy.wait()
    for h, c in enumerate(copies):
        c.wait()

        def plane(x, carry):
            for b in range(2):
                lanes = slice(128 * b, 128 * b + 128)
                table = table_all[x, pl.ds(b, BY, stride=2), :]

                def pop(i):
                    return raw[i, x, :, lanes].astype(F32) * jnp.broadcast_to(table[:, i : i + 1], (BY, 128))

                def store(axis, value):
                    vel[axis, x, :, lanes] = value

                plane_velocity(pop, store)
            return carry

        lax.fori_loop(4 * h, 4 * h + 4, plane, 0)
    yield


def late_velocities(pops, scale, adj, solid_in, vel, ext, solid, raw, table_all, sems):
    work = velocity_planes(pops, scale, 1, vel, raw, table_all, sems)
    next(work)
    adj_copy = pltpu.make_async_copy(adj, ext.at[:, pl.ds(2, BX)], sems.at[3])
    adj_copy.start()
    solid_copy = pltpu.make_async_copy(solid_in, solid, sems.at[4])
    solid_copy.start()
    next(work)
    adj_copy.wait()
    solid_copy.wait()


def early_velocities(pops, scale, after, vel, raw, table_all, sems):
    del after
    work = velocity_planes(pops, scale, 0, vel, raw, table_all, sems)
    next(work)
    next(work)


def held(i, x):
    if x in (0, EX - 1):
        return VEL[i][0] == (-1 if x == 0 else 1)
    if x in (1, EX - 2):
        return VEL[i][0] in (0, -1 if x == 1 else 1)
    return True


def regroup(left, own, right, after, down, same, up):
    del after
    gx = lax.axis_index("gx")
    a = jnp.where(gx > 0, left[...], 0.0)
    b = own[...]
    c = jnp.where(gx < lax.axis_size("gx") - 1, right[...], 0.0)
    lane = iota((24, 128), 1)
    for j, out in enumerate((down, same, up)):
        ra = pltpu.roll(a, (-LIST * j) % 128, 1)
        rb = pltpu.roll(b, (LIST - LIST * j) % 128, 1)
        rc = pltpu.roll(c, (2 * LIST - LIST * j) % 128, 1)
        out[...] = jnp.where(
            lane < LIST, ra, jnp.where(lane < 2 * LIST, rb, jnp.where(lane < 3 * LIST, rc, 0.0))
        )


Y_ROWS = 23 * EX + 4


def put(entry, x):
    return slice(EX * entry + x, EX * entry + x + 1)


def y_faces(ext_in, from_left, from_right, vel, solid, ext, to_down, to_up):
    del ext_in
    gx = lax.axis_index("gx")
    in_left, in_right = gx > 0, gx < lax.axis_size("gx") - 1
    for sign, ref, ok, near_x, far_x in ((-1, from_left, in_left, 1, 0), (1, from_right, in_right, 10, 11)):
        near, far = face_rows(0, sign)
        for slot, i in enumerate(near):
            ext[i, near_x] = jnp.where(ok, ref[slot], 0.0)
        for slot, i in enumerate(far):
            ext[i, far_x] = jnp.where(ok, ref[14 + slot], 0.0)
    for sign, out, near_y, far_y in ((1, to_down, 0, 1), (-1, to_up, BY - 1, BY - 2)):
        near, far = face_rows(1, sign)
        out[...] = jnp.zeros((Y_ROWS, BZ), F32)
        for base, pops, y in ((0, near, near_y), (14, far, far_y)):
            for slot, i in enumerate(pops):
                for x in range(EX):
                    if held(i, x):
                        out[put(base + slot, x), :] = ext[i, x, y : y + 1, :]
        for row in range(19, 23):
            out[put(row, 1), :] = from_left[row, near_y : near_y + 1, :]
            out[put(row, 10), :] = from_right[row, near_y : near_y + 1, :]
        for x in range(BX):
            for axis in range(3):
                out[put(19 + axis, x + 2), :] = vel[axis, x, near_y : near_y + 1, :]
            out[put(22, x + 2), :] = (solid[x, near_y : near_y + 1, :] > 0).astype(F32)


def halves(v):
    hi = v.astype(jnp.bfloat16)
    return hi, (v - hi.astype(F32)).astype(jnp.bfloat16)


def one_hot(rows, targets):
    return (iota((rows, targets.shape[1]), 0) == targets).astype(F32).astype(jnp.bfloat16)


def contract_lanes(a, b):
    return lax.dot_general(a, b, (((1,), (1,)), ((), ())), preferred_element_type=F32)


def scatter(ext_in, down, same, up, vel, solid, ext, to_left, to_right, merged, where_xy, where_z):
    del ext_in
    gy = lax.axis_index("gy")
    merged[:, 0:128] = jnp.where(gy > 0, down[...], 0.0)
    merged[:, 128:256] = same[...]
    merged[:, 256:384] = jnp.where(gy < lax.axis_size("gy") - 1, up[...], 0.0)
    cell = merged[19:20, :].astype(jnp.int32)
    where_xy[...] = one_hot(128, cell // BZ)
    where_z[...] = one_hot(BZ, cell % BZ)
    for i in range(19):
        hi, lo = halves(merged[i : i + 1, :])
        rows = where_xy[...]
        field = contract_lanes(jnp.concatenate([rows * hi, rows * lo], axis=0), where_z[...])
        ext[i, 2 : 2 + BX] = ext[i, 2 : 2 + BX] + (field[0:128] + field[128:256]).reshape(BX, BY, BZ)
    for sign, out, near_x, far_x in ((1, to_left, 2, 3), (-1, to_right, 9, 8)):
        near, far = face_rows(0, sign)
        for slot, i in enumerate(near):
            out[slot] = ext[i, near_x]
        for slot, i in enumerate(far):
            out[14 + slot] = ext[i, far_x]
        for axis in range(3):
            out[19 + axis] = vel[axis, near_x - 2]
        out[22] = (solid[near_x - 2] > 0).astype(F32)


def adjoint_collide(u, is_solid, r, want):
    square = u[0] * u[0] + u[1] * u[1] + u[2] * u[2]
    axis_sum = diag_sum = axis_quad = diag_quad = None
    axis_mom = [None, None, None]
    diag_mom = [None, None, None]

    def plus(a, b):
        return b if a is None else a + b

    for n, (ip, im, c) in enumerate(PAIRS):
        s, d = r[ip] + r[im], r[ip] - r[im]
        p = None
        for axis in range(3):
            if c[axis]:
                p = u[axis] if p is None else (p + u[axis] if c[axis] > 0 else p - u[axis])
        q = p * s
        m = d + 3.0 * q
        if n < 3:
            axis_sum, axis_quad = plus(axis_sum, s), plus(axis_quad, q * p)
            axis_mom[n] = m
        else:
            diag_sum, diag_quad = plus(diag_sum, s), plus(diag_quad, q * p)
            for axis in range(3):
                if c[axis] > 0:
                    diag_mom[axis] = plus(diag_mom[axis], m)
                elif c[axis] < 0:
                    diag_mom[axis] = diag_mom[axis] - m
    scale = 1.0 / RELAX
    keep = 1.0 - scale
    total = (scale / 3.0) * r[0] + (scale / 18.0) * axis_sum + (scale / 36.0) * diag_sum
    quad = (4.5 * scale / 18.0) * axis_quad + (4.5 * scale / 36.0) * diag_quad
    density = total * (1.0 + 1.5 * square) - quad
    triple = 3.0 * total
    grad = [
        (3.0 * scale / 18.0) * axis_mom[a] + (3.0 * scale / 36.0) * diag_mom[a] - triple * u[a] for a in range(3)
    ]
    out = {}
    if 0 in want:
        out[0] = jnp.where(is_solid, r[0], keep * r[0] + density)
    for ip, im, c in PAIRS:
        if ip not in want and im not in want:
            continue
        g = None
        for axis in range(3):
            if c[axis]:
                g = grad[axis] if g is None else (g + grad[axis] if c[axis] > 0 else g - grad[axis])
        if ip in want:
            out[ip] = jnp.where(is_solid, r[im], keep * r[ip] + (density + g))
        if im in want:
            out[im] = jnp.where(is_solid, r[ip], keep * r[im] + (density - g))
    return out


def shift_z(v, step):
    if step == 0:
        return v
    lane = iota(v.shape, 1)
    if step > 0:
        return jnp.where(lane == BZ - 1, 0.0, pltpu.roll(v, BZ - 1, 1))
    return jnp.where(lane == 0, 0.0, pltpu.roll(v, 1, 1))


def read_plane(field, low_face, high_face, x, i, low_slot, high_slot):
    cx, cy, cz = VEL[i]
    v = field[i, x + cx]
    if cy:
        row = iota(v.shape, 0)
        if cy > 0:
            edge = high_face[high_slot[i], pl.ds(x + cx, 1), :]
            v = jnp.where(row == BY - 1, jnp.broadcast_to(edge, v.shape), pltpu.roll(v, BY - 1, 0))
        else:
            edge = low_face[low_slot[i], pl.ds(x + cx, 1), :]
            v = jnp.where(row == 0, jnp.broadcast_to(edge, v.shape), pltpu.roll(v, 1, 0))
    return shift_z(v, cz)


def collide_block(reads, load_u, load_solid, want, store):
    for h in range(2):
        for b in range(2):
            rows, lanes = slice(8 * h, 8 * h + 8), slice(128 * b, 128 * b + 128)
            r = [reads[i, rows, lanes] for i in range(19)]
            u = [load_u(axis, rows, lanes) for axis in range(3)]
            out = adjoint_collide(u, load_solid(rows, lanes), r, want)
            for i in want:
                store(i, rows, lanes, out[i])


def entry(face, n):
    return face[EX * n : EX * n + 16, :]


def two_steps(
    ext, from_left, from_right, from_down, from_up, to_down, to_up, vel_late, vel_early, solid,
    initial, middle,
    mid_ext, first, low_near, high_near, low_face, high_face, reads, mid_sems, first_sems,
):
    gx, gy = lax.axis_index("gx"), lax.axis_index("gy")
    in_left, in_right = gx > 0, gx < lax.axis_size("gx") - 1
    in_down, in_up = gy > 0, gy < lax.axis_size("gy") - 1

    for n in range(14):
        low_near[n] = jnp.where(in_down, entry(from_down, n), 0.0)
        high_near[n] = jnp.where(in_up, entry(from_up, n), 0.0)

    for x, ref, ok, sign in ((1, from_left, in_left, -1), (EX - 2, from_right, in_right, 1)):
        for i in range(19):
            reads[i] = read_plane(ext, low_near, high_near, x, i, NEAR_DOWN, NEAR_UP)

        def keep(i, rows, lanes, value, x=x, ok=ok):
            mid_ext[i, x, rows, lanes] = jnp.where(ok, value, 0.0)

        collide_block(
            reads,
            lambda axis, rows, lanes, ref=ref: ref[19 + axis, rows, lanes],
            lambda rows, lanes, ref=ref: ref[22, rows, lanes] > 0.0,
            face_rows(0, sign)[1],
            keep,
        )

    for ref, mine, mine_slot, near, far, sign, ok, out in (
        (from_down, to_down, NEAR_UP, NEAR_DOWN, FAR_DOWN, -1, in_down, low_face),
        (from_up, to_up, NEAR_DOWN, NEAR_UP, FAR_UP, 1, in_up, high_face),
    ):
        for i in range(19):
            cx, cy, cz = VEL[i]
            if cy == 0:
                v = entry(ref, near[i])
            elif cy == sign:
                v = entry(ref, 14 + far[i])
            else:
                v = entry(mine, mine_slot[i])
            if cx:
                v = pltpu.roll(v, (-cx) % 16, 0)
            reads[i] = shift_z(v, cz)
        row = iota((8, 128), 0)

        def keep_row(i, rows, lanes, value, out=out, far=far, ok=ok):
            x = row + rows.start
            good = ok & ((x > 1) | in_left) & ((x < EX - 2) | in_right)
            out[far[i], rows, lanes] = jnp.where(good, value, 0.0)

        collide_block(
            reads,
            lambda axis, rows, lanes, ref=ref: entry(ref, 19 + axis)[rows, lanes],
            lambda rows, lanes, ref=ref: entry(ref, 22)[rows, lanes] > 0.0,
            face_rows(1, sign)[1],
            keep_row,
        )

    def mid_copy(x):
        return pltpu.make_async_copy(mid_ext.at[:, pl.ds(x + 2, 1)], middle.at[:, pl.ds(x, 1)], mid_sems.at[x])

    def first_copy(x):
        return pltpu.make_async_copy(first.at[:, pl.ds(x, 1)], initial.at[:, pl.ds(x, 1)], first_sems.at[x])

    def mid_plane(x, carry):
        for i in range(19):
            reads[i] = read_plane(ext, low_near, high_near, x + 2, i, NEAR_DOWN, NEAR_UP)

        def keep(i, rows, lanes, value):
            mid_ext[i, x + 2, rows, lanes] = value

        collide_block(
            reads,
            lambda axis, rows, lanes: vel_late[axis, x, rows, lanes],
            lambda rows, lanes: solid[x, rows, lanes] > 0,
            ALL,
            keep,
        )
        mid_copy(x).start()
        return carry

    lax.fori_loop(0, BX, mid_plane, 0)

    def first_plane(x, carry):
        for i in range(19):
            reads[i] = read_plane(mid_ext, low_face, high_face, x + 2, i, FAR_DOWN, FAR_UP)

        def keep(i, rows, lanes, value):
            first[i, x, rows, lanes] = value

        collide_block(
            reads,
            lambda axis, rows, lanes: vel_early[axis, x, rows, lanes],
            lambda rows, lanes: solid[x, rows, lanes] > 0,
            ALL,
            keep,
        )
        first_copy(x).start()
        return carry

    lax.fori_loop(0, BX, first_plane, 0)

    def finish(x, carry):
        mid_copy(x).wait()
        first_copy(x).wait()
        return carry

    lax.fori_loop(0, BX, finish, 0)


def shifted(value, axis, step):
    count = lax.axis_size(axis)
    return lax.ppermute(value, axis, [(i, (i + step) % count) for i in range(count)])


def body(adj_later, saved_pops, saved_scale, solid, seed_values, seed_contact, seed_cell):
    adj, pops, solid_h = in_hbm(adj_later), in_hbm(saved_pops), in_hbm(solid)
    scale = in_hbm(saved_scale.transpose(0, 2, 3, 4, 1).reshape(2, BX, 2 * BY, 19))
    block = pltpu.VMEM((24, 128), F32)
    x_face = pltpu.VMEM((23, BY, BZ), F32)
    y_face = pltpu.VMEM((Y_ROWS, BZ), F32)
    extended = pltpu.VMEM((19, EX, BY, BZ), F32)
    flow = pltpu.VMEM((3, BX, BY, BZ), F32)
    low, mid, high = call(
        group_items,
        (block,) * 3,
        [hbm] * 3,
        (in_hbm(seed_values.T), in_hbm(seed_contact.reshape(1, 128)), in_hbm(seed_cell.reshape(1, 128))),
        scratch=[
            pltpu.VMEM((24, 128), F32),
            pltpu.VMEM((19, 128), F32),
            pltpu.VMEM((1, 128), jnp.int32),
            pltpu.VMEM((1, 128), jnp.int32),
            pltpu.SemaphoreType.DMA((3,)),
        ],
    )
    left = in_vmem(shifted(high, "gx", 1))
    right = in_vmem(shifted(low, "gx", -1))

    raw = pltpu.VMEM((19, BX, BY, BZ), jnp.bfloat16)
    table = pltpu.VMEM((BX, 2 * BY, 19), F32)
    vel_late, ext, solid_v = call(
        late_velocities,
        (flow, extended, pltpu.VMEM((BX, BY, BZ), jnp.int32)),
        [hbm] * 4,
        (pops, scale, adj, solid_h),
        scratch=[raw, table, pltpu.SemaphoreType.DMA((5,))],
    )
    down, same, up = call(regroup, (block,) * 3, [vmem] * 4, (left, mid, right, solid_v))
    from_low = in_vmem(shifted(up, "gy", 1))
    from_high = in_vmem(shifted(down, "gy", -1))
    vel_early = call(
        early_velocities, flow, [hbm, hbm, vmem], (pops, scale, same),
        scratch=[raw, table, pltpu.SemaphoreType.DMA((3,))],
    )
    ext, to_left, to_right = call(
        scatter,
        (extended, x_face, x_face),
        [vmem] * 6,
        (ext, from_low, same, from_high, vel_late, solid_v),
        scratch=[
            pltpu.VMEM((24, 384), F32), pltpu.VMEM((128, 384), jnp.bfloat16), pltpu.VMEM((BZ, 384), jnp.bfloat16),
        ],
        aliases={0: 0},
    )
    from_left = in_vmem(shifted(to_right, "gx", 1))
    from_right = in_vmem(shifted(to_left, "gx", -1))
    ext, to_down, to_up = call(
        y_faces,
        (extended, y_face, y_face),
        [vmem] * 5,
        (ext, from_left, from_right, vel_late, solid_v),
        aliases={0: 0},
    )
    from_down = in_vmem(shifted(to_up, "gy", 1))
    from_up = in_vmem(shifted(to_down, "gy", -1))
    field = jax.ShapeDtypeStruct((19, BX, BY, BZ), F32)
    return call(
        two_steps,
        (field, field),
        [vmem] * 10,
        (ext, from_left, from_right, from_down, from_up, to_down, to_up, vel_late, vel_early, solid_v),
        scratch=[
            pltpu.VMEM((19, EX, BY, BZ), F32),
            pltpu.VMEM((19, BX, BY, BZ), F32),
            pltpu.VMEM((14, 16, BZ), F32),
            pltpu.VMEM((14, 16, BZ), F32),
            pltpu.VMEM((5, 16, BZ), F32),
            pltpu.VMEM((5, 16, BZ), F32),
            pltpu.VMEM((19, BY, BZ), F32),
            pltpu.SemaphoreType.DMA((BX,)),
            pltpu.SemaphoreType.DMA((BX,)),
        ],
    )


def solution(mesh):
    return jax.shard_map(
        body,
        mesh=mesh,
        in_specs=(
            P(None, "gx", "gy", None),
            P(None, None, "gx", "gy", None),
            P(None, None, "gx", "gy", None),
            P("gx", "gy", None),
            P(("gx", "gy"), None),
            P(("gx", "gy"), None),
            P(("gx", "gy")),
        ),
        out_specs=(P(None, "gx", "gy", None), P(None, "gx", "gy", None)),
        check_vma=False,
    )
```

time: 52.8 us -> 46.1 us (0.87)
  local copies, waits for them, and re-layouts: 6.37 us -> 0 us
  Pallas kernels: 9.99 us -> 13.3 us
  waiting for transfers between devices: 16.4 us -> 14.1 us
  starting transfers between devices: 19.1 us -> 17.7 us
    unnamed x14 -> x0, local copies, waits for them, and re-layouts: 6.37 us -> none
    pallas_call x6 -> x7, Pallas kernels: 9.99 us -> 13.3 us  [call(): pl.pallas_call(body, out_shape=outs, in_specs=in_specs, out_specs=out_spe...]
    ppermute x8, waiting for transfers between devices: 16.4 us -> 14.1 us  [shifted(): lax.ppermute(value, axis, [(i, (i + step) % count) for i in range(count)])]
    ppermute x8, starting transfers between devices: 19.1 us -> 17.7 us  [shifted(): lax.ppermute(value, axis, [(i, (i + step) % count) for i in range(count)])]
  transfers between devices with their start and end apart: 8 -> 8, of which waited for: 5 -> 5; matrix products, arithmetic and copies ran while one was open for 0% -> 0% of each run, Pallas kernels for 7% -> 12%
where the time goes in v2:
time: 46.1 us; the launch traced here: 45.8 us
  starting transfers between devices  17.7 us (38%)
  waiting for transfers between devices  14.1 us (31%)
  Pallas kernels  13.3 us (29%)
  between operations  0.71 us (2%)
    ppermute x8, starting transfers between devices, shifted(): lax.ppermute(value, axis, [(i, (i + step) % count) for i in range(count)])  17.7 us
    ppermute x8, waiting for transfers between devices, shifted(): lax.ppermute(value, axis, [(i, (i + step) % count) for i in range(count)])  14.1 us
    pallas_call x7, Pallas kernels, call(): pl.pallas_call(body, out_shape=outs, in_specs=in_specs, out_specs=out_spe...  13.3 us
  transfers between devices with their start and end apart: 8, of which 5 were waited for; matrix products, arithmetic and copies ran while one was open for 0% of the time, Pallas kernels for 12%

profile of v2, /device:TPU:6, one launch (start us, length us, event | category | flops | bytes accessed | tf_op | source)
XLA Modules:
  0.0 45.8 jit_solution(17985318930627297499)
XLA Ops:
  0.6 1.3 %shard_map.87 = (f32[24,128]{1,0:T(8,128)S(1)}, f32[24,128]{1,0:T(8,128)S(1)}, f32[24,128]{1,0:T(8,128)S(1)}) custom-call(f32[19,128]{1,0:T(8,128)} %bitcast.8, s32[1,128]{1,0:T(1,128)} %bitcast.9, s32[1,128]{1,0:T(1,128)} %bitcast.10), custom_call_target="tpu_custom_call" | custom-call | tf_op jit(solution)/shard_map/pallas_call | solution.py:60
  2.0 0.1 collective-permute-start
  2.1 8.0 %collective-permute-start.1 = (f32[24,128]{1,0:T(8,128)S(1)}, f32[24,128]{1,0:T(8,128)S(1)}, u32[]{:S(2)}, u32[]{:S(2)}) collective-permute-start(f32[24,128]{1,0:T(8,128)S(1)} %get-tuple-element.20), channel_id=1, source_target_pairs={{0,248},{8,0},{16,8},{24,16},{32,24},{40,32},{48,40},{56,48},{64,5... | collective-permute-start | bytes 36872 | tf_op jit(solution)/shard_map/ppermute | solution.py:479
  10.1 2.8 %shard_map.86 = (f32[3,8,16,256]{3,2,1,0:T(8,128)S(1)}, f32[19,12,16,256]{3,2,1,0:T(8,128)S(1)}, s32[8,16,256]{2,1,0:T(8,128)S(1)}) custom-call(bf16[2,19,8,16,256]{4,3,2,1,0:T(8,128)(2,1)} %pops.3, f32[2,8,32,19]{3,2,1,0:T(8,128)} %bitcast.6, f32[19,8,16,256]{3,2,1,0:T(8,128)} %adj.1, s32[8,16,256]{2,1,0:T(8,128)} %solid_in.1), custom_call_target="tpu_custom_call" | custom-call | tf_op jit(solution)/shard_map/pallas_call | solution.py:60
  12.9 0.0 collective-permute-done.left
  12.9 0.0 collective-permute-done.1.right
  12.9 0.1 shard_map.88
  13.0 0.7 %collective-permute-start.2 = (f32[24,128]{1,0:T(8,128)S(1)}, f32[24,128]{1,0:T(8,128)S(1)}, u32[]{:S(2)}, u32[]{:S(2)}) collective-permute-start(f32[24,128]{1,0:T(8,128)S(1)} %get-tuple-element.22), channel_id=1, source_target_pairs={{0,1},{1,2},{2,3},{3,4},{4,5},{5,6},{6,7},{7,0},{8,9},{9,10},{10,1... | collective-permute-start | bytes 36872 | tf_op jit(solution)/shard_map/ppermute | solution.py:479
  13.7 1.4 %collective-permute-start.3 = (f32[24,128]{1,0:T(8,128)S(1)}, f32[24,128]{1,0:T(8,128)S(1)}, u32[]{:S(2)}, u32[]{:S(2)}) collective-permute-start(f32[24,128]{1,0:T(8,128)S(1)} %get-tuple-element.24), channel_id=1, source_target_pairs={{0,7},{1,0},{2,1},{3,2},{4,3},{5,4},{6,5},{7,6},{8,15},{9,8},{10,9... | collective-permute-start | bytes 36872 | tf_op jit(solution)/shard_map/ppermute | solution.py:479
  15.1 1.7 %collective-permute-done.2.down = f32[24,128]{1,0:T(8,128)S(1)} collective-permute-done((f32[24,128]{1,0:T(8,128)S(1)}, f32[24,128]{1,0:T(8,128)S(1)}, u32[]{:S(2)}, u32[]{:S(2)}) %collective-permute-start.2) | collective-permute-done | bytes 12320 | tf_op jit(solution)/shard_map/ppermute | solution.py:479
  16.8 2.7 %collective-permute-done.3.up = f32[24,128]{1,0:T(8,128)S(1)} collective-permute-done((f32[24,128]{1,0:T(8,128)S(1)}, f32[24,128]{1,0:T(8,128)S(1)}, u32[]{:S(2)}, u32[]{:S(2)}) %collective-permute-start.3) | collective-permute-done | bytes 12320 | tf_op jit(solution)/shard_map/ppermute | solution.py:479
  19.5 1.5 %shard_map.89 = (f32[19,12,16,256]{3,2,1,0:T(8,128)S(1)}, f32[23,16,256]{2,1,0:T(8,128)S(1)}, f32[23,16,256]{2,1,0:T(8,128)S(1)}) custom-call(f32[19,12,16,256]{3,2,1,0:T(8,128)S(1)} %get-tuple-element.17.ext_in, f32[24,128]{1,0:T(8,128)S(1)} %collective-permute-done.2.down, ...), custom_call_target="tpu_custom_call", output_to_operand_aliasing={{0}: (0, {})} | custom-call | tf_op jit(solution)/shard_map/pallas_call | solution.py:60
  21.0 0.1 collective-permute-start.4
  21.1 5.3 %collective-permute-start.5 = (f32[23,16,256]{2,1,0:T(8,128)S(1)}, f32[23,16,256]{2,1,0:T(8,128)S(1)}, u32[]{:S(2)}, u32[]{:S(2)}) collective-permute-start(f32[23,16,256]{2,1,0:T(8,128)S(1)} %get-tuple-element.28), channel_id=1, source_target_pairs={{0,248},{8,0},{16,8},{24,16},{32,24},{40,32},{48,40},{56,48},{64,5... | collective-permute-start | bytes 1130504 | tf_op jit(solution)/shard_map/ppermute | solution.py:479
  26.5 5.4 %collective-permute-done.4.from_left = f32[23,16,256]{2,1,0:T(8,128)S(1)} collective-permute-done((f32[23,16,256]{2,1,0:T(8,128)S(1)}, f32[23,16,256]{2,1,0:T(8,128)S(1)}, u32[]{:S(2)}, u32[]{:S(2)}) %collective-permute-start.4) | collective-permute-done | bytes 376864 | tf_op jit(solution)/shard_map/ppermute | solution.py:479
  31.9 0.0 collective-permute-done.5.from_right
  31.9 0.3 shard_map.90
  32.2 0.5 %collective-permute-start.6 = (f32[280,256]{1,0:T(8,128)S(1)}, f32[280,256]{1,0:T(8,128)S(1)}, u32[]{:S(2)}, u32[]{:S(2)}) collective-permute-start(f32[280,256]{1,0:T(8,128)S(1)} %get-tuple-element.30.to_up), channel_id=1, source_target_pairs={{0,1},{1,2},{2,3},{3,4},{4,5},{5,6},{6,7},{7,0},{8,9},{9,10},{10,1... | collective-permute-start | bytes 860168 | tf_op jit(solution)/shard_map/ppermute | solution.py:479
  32.7 1.6 %collective-permute-start.7 = (f32[280,256]{1,0:T(8,128)S(1)}, f32[280,256]{1,0:T(8,128)S(1)}, u32[]{:S(2)}, u32[]{:S(2)}) collective-permute-start(f32[280,256]{1,0:T(8,128)S(1)} %get-tuple-element.31.to_down), channel_id=1, source_target_pairs={{0,7},{1,0},{2,1},{3,2},{4,3},{5,4},{6,5},{7,6},{8,15},{9,8},{10,9... | collective-permute-start | bytes 860168 | tf_op jit(solution)/shard_map/ppermute | solution.py:479
  34.3 2.8 %shard_map.91.vel_early = f32[3,8,16,256]{3,2,1,0:T(8,128)S(1)} custom-call(bf16[2,19,8,16,256]{4,3,2,1,0:T(8,128)(2,1)} %pops.3, f32[2,8,32,19]{3,2,1,0:T(8,128)} %bitcast.7, f32[24,128]{1,0:T(8,128)S(1)} %get-tuple-element.23.same.after), custom_call_target="tpu_custom_call" | custom-call | tf_op jit(solution)/shard_map/pallas_call | solution.py:60
  37.1 1.8 %collective-permute-done.6.from_down = f32[280,256]{1,0:T(8,128)S(1)} collective-permute-done((f32[280,256]{1,0:T(8,128)S(1)}, f32[280,256]{1,0:T(8,128)S(1)}, u32[]{:S(2)}, u32[]{:S(2)}) %collective-permute-start.6) | collective-permute-done | bytes 286752 | tf_op jit(solution)/shard_map/ppermute | solution.py:479
  38.9 2.5 %collective-permute-done.7.from_up = f32[280,256]{1,0:T(8,128)S(1)} collective-permute-done((f32[280,256]{1,0:T(8,128)S(1)}, f32[280,256]{1,0:T(8,128)S(1)}, u32[]{:S(2)}, u32[]{:S(2)}) %collective-permute-start.7) | collective-permute-done | bytes 286752 | tf_op jit(solution)/shard_map/ppermute | solution.py:479
  41.4 4.4 %shard_map.92 = (f32[19,8,16,256]{3,2,1,0:T(8,128)}, f32[19,8,16,256]{3,2,1,0:T(8,128)}) custom-call(f32[19,12,16,256]{3,2,1,0:T(8,128)S(1)} %get-tuple-element.29.ext, f32[23,16,256]{2,1,0:T(8,128)S(1)} %collective-permute-done.4.from_left, f32[23,16,256]{2,1,0:T(8,128)S(1)} %collective-permute-done.5.from_right, ...), custom_call_target="tpu_custom_call" | custom-call | tf_op jit(solution)/shard_map/pallas_call | solution.py:60
Async XLA Ops:
  2.0 10.9 %collective-permute-start = (f32[24,128]{1,0:T(8,128)S(1)}, f32[24,128]{1,0:T(8,128)S(1)}, u32[]{:S(2)}, u32[]{:S(2)}) collective-permute-start(f32[24,128]{1,0:T(8,128)S(1)} %get-tuple-element.18), channel_id=1, source_target_pairs={{0,8},{8,16},{16,24},{24,32},{32,40},{40,48},{48,56},{56,64},{64,7... | collective-permute-start | bytes 36872 | tf_op jit(solution)/shard_map/ppermute | solution.py:479
  2.1 10.8 %collective-permute-start.1 = (f32[24,128]{1,0:T(8,128)S(1)}, f32[24,128]{1,0:T(8,128)S(1)}, u32[]{:S(2)}, u32[]{:S(2)}) collective-permute-start(f32[24,128]{1,0:T(8,128)S(1)} %get-tuple-element.20), channel_id=1, source_target_pairs={{0,248},{8,0},{16,8},{24,16},{32,24},{40,32},{48,40},{56,48},{64,5... | collective-permute-start | bytes 36872 | tf_op jit(solution)/shard_map/ppermute | solution.py:479
  13.0 3.8 %collective-permute-start.2 = (f32[24,128]{1,0:T(8,128)S(1)}, f32[24,128]{1,0:T(8,128)S(1)}, u32[]{:S(2)}, u32[]{:S(2)}) collective-permute-start(f32[24,128]{1,0:T(8,128)S(1)} %get-tuple-element.22), channel_id=1, source_target_pairs={{0,1},{1,2},{2,3},{3,4},{4,5},{5,6},{6,7},{7,0},{8,9},{9,10},{10,1... | collective-permute-start | bytes 36872 | tf_op jit(solution)/shard_map/ppermute | solution.py:479
  13.7 5.8 %collective-permute-start.3 = (f32[24,128]{1,0:T(8,128)S(1)}, f32[24,128]{1,0:T(8,128)S(1)}, u32[]{:S(2)}, u32[]{:S(2)}) collective-permute-start(f32[24,128]{1,0:T(8,128)S(1)} %get-tuple-element.24), channel_id=1, source_target_pairs={{0,7},{1,0},{2,1},{3,2},{4,3},{5,4},{6,5},{7,6},{8,15},{9,8},{10,9... | collective-permute-start | bytes 36872 | tf_op jit(solution)/shard_map/ppermute | solution.py:479
  21.0 10.8 %collective-permute-start.4 = (f32[23,16,256]{2,1,0:T(8,128)S(1)}, f32[23,16,256]{2,1,0:T(8,128)S(1)}, u32[]{:S(2)}, u32[]{:S(2)}) collective-permute-start(f32[23,16,256]{2,1,0:T(8,128)S(1)} %get-tuple-element.27), channel_id=1, source_target_pairs={{0,8},{8,16},{16,24},{24,32},{32,40},{40,48},{48,56},{56,64},{64,7... | collective-permute-start | bytes 1130504 | tf_op jit(solution)/shard_map/ppermute | solution.py:479
  21.1 10.8 %collective-permute-start.5 = (f32[23,16,256]{2,1,0:T(8,128)S(1)}, f32[23,16,256]{2,1,0:T(8,128)S(1)}, u32[]{:S(2)}, u32[]{:S(2)}) collective-permute-start(f32[23,16,256]{2,1,0:T(8,128)S(1)} %get-tuple-element.28), channel_id=1, source_target_pairs={{0,248},{8,0},{16,8},{24,16},{32,24},{40,32},{48,40},{56,48},{64,5... | collective-permute-start | bytes 1130504 | tf_op jit(solution)/shard_map/ppermute | solution.py:479
  32.2 6.7 %collective-permute-start.6 = (f32[280,256]{1,0:T(8,128)S(1)}, f32[280,256]{1,0:T(8,128)S(1)}, u32[]{:S(2)}, u32[]{:S(2)}) collective-permute-start(f32[280,256]{1,0:T(8,128)S(1)} %get-tuple-element.30.to_up), channel_id=1, source_target_pairs={{0,1},{1,2},{2,3},{3,4},{4,5},{5,6},{6,7},{7,0},{8,9},{9,10},{10,1... | collective-permute-start | bytes 860168 | tf_op jit(solution)/shard_map/ppermute | solution.py:479
  32.7 8.7 %collective-permute-start.7 = (f32[280,256]{1,0:T(8,128)S(1)}, f32[280,256]{1,0:T(8,128)S(1)}, u32[]{:S(2)}, u32[]{:S(2)}) collective-permute-start(f32[280,256]{1,0:T(8,128)S(1)} %get-tuple-element.31.to_down), channel_id=1, source_target_pairs={{0,7},{1,0},{2,1},{3,2},{4,3},{5,4},{6,5},{7,6},{8,15},{9,8},{10,9... | collective-permute-start | bytes 860168 | tf_op jit(solution)/shard_map/ppermute | solution.py:479

commit v3 on v2

--- a/solution.py
+++ b/solution.py
@@ -115,7 +115,7 @@
     counts = jnp.dot(hot, before, preferred_element_type=F32)
     rank = jnp.sum(jnp.where(iota((16, 128), 0) == code, counts, 0.0), axis=0, keepdims=True).astype(jnp.int32)
     third = (code >= 3).astype(jnp.int32) + (code >= 6).astype(jnp.int32)
-    slot = third * 128 + (code - 3 * third) * LIST + rank
+    slot = (code - 3 * third) * 128 + third * LIST + rank
     pay[...] = jnp.zeros((24, 128), F32)
     pay[0:19, :] = own_values[...]
     pay[19:20, :] = own_cell[...].astype(F32)
@@ -185,14 +185,14 @@
     return True
 
 
-def regroup(left, own, right, after, down, same, up):
+def regroup(below, own, above, after, west, here, east):
     del after
-    gx = lax.axis_index("gx")
-    a = jnp.where(gx > 0, left[...], 0.0)
+    gy = lax.axis_index("gy")
+    a = jnp.where(gy > 0, below[...], 0.0)
     b = own[...]
-    c = jnp.where(gx < lax.axis_size("gx") - 1, right[...], 0.0)
+    c = jnp.where(gy < lax.axis_size("gy") - 1, above[...], 0.0)
     lane = iota((24, 128), 1)
-    for j, out in enumerate((down, same, up)):
+    for j, out in enumerate((west, here, east)):
         ra = pltpu.roll(a, (-LIST * j) % 128, 1)
         rb = pltpu.roll(b, (LIST - LIST * j) % 128, 1)
         rc = pltpu.roll(c, (2 * LIST - LIST * j) % 128, 1)
@@ -208,16 +208,90 @@
     return slice(EX * entry + x, EX * entry + x + 1)
 
 
-def y_faces(ext_in, from_left, from_right, vel, solid, ext, to_down, to_up):
+def halves(v):
+    hi = v.astype(jnp.bfloat16)
+    return hi, (v - hi.astype(F32)).astype(jnp.bfloat16)
+
+
+def one_hot(rows, targets):
+    return (iota((rows, targets.shape[1]), 0) == targets).astype(F32).astype(jnp.bfloat16)
+
+
+def contract_lanes(a, b):
+    return lax.dot_general(a, b, (((1,), (1,)), ((), ())), preferred_element_type=F32)
+
+
+def add_own(ext, items, where_xy, where_z):
+    cell = items[19:20, :].astype(jnp.int32)
+    where_xy[...] = one_hot(128, cell // BZ)
+    where_z[...] = one_hot(BZ, cell % BZ)
+    for i in range(19):
+        hi, lo = halves(items[i : i + 1, :])
+        rows = where_xy[...]
+        field = contract_lanes(jnp.concatenate([rows * hi, rows * lo], axis=0), where_z[...])
+        ext[i, 2 : 2 + BX] = ext[i, 2 : 2 + BX] + (field[0:128] + field[128:256]).reshape(BX, BY, BZ)
+
+
+def own_seeds(ext_in, west, here, east, vel, solid, ext, to_left, to_right, where_xy, where_z):
     del ext_in
-    gx = lax.axis_index("gx")
-    in_left, in_right = gx > 0, gx < lax.axis_size("gx") - 1
-    for sign, ref, ok, near_x, far_x in ((-1, from_left, in_left, 1, 0), (1, from_right, in_right, 10, 11)):
+    add_own(ext, here, where_xy, where_z)
+    for sign, out, items, near_x, far_x in ((1, to_left, west, 2, 3), (-1, to_right, east, 9, 8)):
         near, far = face_rows(0, sign)
         for slot, i in enumerate(near):
-            ext[i, near_x] = jnp.where(ok, ref[slot], 0.0)
+            out[slot] = ext[i, near_x]
         for slot, i in enumerate(far):
-            ext[i, far_x] = jnp.where(ok, ref[14 + slot], 0.0)
+            out[14 + slot] = ext[i, far_x]
+        for axis in range(3):
+            out[19 + axis] = vel[axis, near_x - 2]
+        out[22] = (solid[near_x - 2] > 0).astype(F32)
+        out[23, :, 0:128] = items[0:16, :]
+        out[23, 0:8, 128:256] = items[16:24, :]
+        out[23, 8:16, 128:256] = jnp.zeros((8, 128), F32)
+
+
+def halo_scatter(items, near_rows, near_target, far_rows, far_target, height, add, stack):
+    near_hot, far_hot = one_hot(16, near_target), one_hot(16, far_target)
+    entries = [(near_hot, i, 0) for i in near_rows] + [(far_hot, i, 1) for i in far_rows]
+    count = len(entries)
+    for n, (hot, i, deep) in enumerate(entries):
+        hi, lo = halves(items[i : i + 1, :])
+        stack[16 * n : 16 * n + 16, :] = hot * hi
+        stack[16 * (count + n) : 16 * (count + n) + 16, :] = hot * lo
+    field = contract_lanes(stack[...], one_hot(BZ, height))
+    for n, (hot, i, deep) in enumerate(entries):
+        add(i, deep, field[16 * n : 16 * n + 16] + field[16 * (count + n) : 16 * (count + n) + 16])
+
+
+def y_faces(
+    ext_in, from_left, from_right, far_left, far_right, west, east, vel, solid,
+    ext, to_down, to_up,
+    items, where_xy, where_z, stack,
+):
+    del ext_in
+    gx, last = lax.axis_index("gx"), lax.axis_size("gx") - 1
+    for n, (face, ok) in enumerate(((from_left, gx > 0), (from_right, gx < last))):
+        lanes = slice(128 * n, 128 * n + 128)
+        items[0:16, lanes] = jnp.where(ok, face[23, :, 0:128], 0.0)
+        items[16:24, lanes] = jnp.where(ok, face[23, 0:8, 128:256], 0.0)
+    add_own(ext, items, where_xy, where_z)
+    for sign, ref, mine, other, ok, other_ok, near_x, far_x, near_cell in (
+        (-1, from_left, west, far_left, gx > 0, gx > 1, 1, 0, BX - 1),
+        (1, from_right, east, far_right, gx < last, gx < last - 1, 10, 11, 0),
+    ):
+        near, far = face_rows(0, sign)
+        slots = {i: n for n, i in enumerate(near)}, {i: 14 + n for n, i in enumerate(far)}
+        items[:, 0:128] = mine[...]
+        items[:, 128:256] = jnp.where(other_ok, other[...], 0.0)
+        cell = items[19:20, :].astype(jnp.int32)
+        x, y = cell // (BY * BZ), (cell // BZ) % BY
+
+        def add(i, deep, field, ref=ref, ok=ok, near_x=near_x, far_x=far_x, slots=slots):
+            ext[i, far_x if deep else near_x] = jnp.where(ok, ref[slots[deep][i]] + field, 0.0)
+
+        halo_scatter(
+            items, near, jnp.where(x == near_cell, y, -1), far, jnp.where(x == near_cell + sign, y, -1),
+            cell % BZ, add, stack,
+        )
     for sign, out, near_y, far_y in ((1, to_down, 0, 1), (-1, to_up, BY - 1, BY - 2)):
         near, far = face_rows(1, sign)
         out[...] = jnp.zeros((Y_ROWS, BZ), F32)
@@ -233,44 +307,6 @@
             for axis in range(3):
                 out[put(19 + axis, x + 2), :] = vel[axis, x, near_y : near_y + 1, :]
             out[put(22, x + 2), :] = (solid[x, near_y : near_y + 1, :] > 0).astype(F32)
-
-
-def halves(v):
-    hi = v.astype(jnp.bfloat16)
-    return hi, (v - hi.astype(F32)).astype(jnp.bfloat16)
-
-
-def one_hot(rows, targets):
-    return (iota((rows, targets.shape[1]), 0) == targets).astype(F32).astype(jnp.bfloat16)
-
-
-def contract_lanes(a, b):
-    return lax.dot_general(a, b, (((1,), (1,)), ((), ())), preferred_element_type=F32)
-
-
-def scatter(ext_in, down, same, up, vel, solid, ext, to_left, to_right, merged, where_xy, where_z):
-    del ext_in
-    gy = lax.axis_index("gy")
-    merged[:, 0:128] = jnp.where(gy > 0, down[...], 0.0)
-    merged[:, 128:256] = same[...]
-    merged[:, 256:384] = jnp.where(gy < lax.axis_size("gy") - 1, up[...], 0.0)
-    cell = merged[19:20, :].astype(jnp.int32)
-    where_xy[...] = one_hot(128, cell // BZ)
-    where_z[...] = one_hot(BZ, cell % BZ)
-    for i in range(19):
-        hi, lo = halves(merged[i : i + 1, :])
-        rows = where_xy[...]
-        field = contract_lanes(jnp.concatenate([rows * hi, rows * lo], axis=0), where_z[...])
-        ext[i, 2 : 2 + BX] = ext[i, 2 : 2 + BX] + (field[0:128] + field[128:256]).reshape(BX, BY, BZ)
-    for sign, out, near_x, far_x in ((1, to_left, 2, 3), (-1, to_right, 9, 8)):
-        near, far = face_rows(0, sign)
-        for slot, i in enumerate(near):
-            out[slot] = ext[i, near_x]
-        for slot, i in enumerate(far):
-            out[14 + slot] = ext[i, far_x]
-        for axis in range(3):
-            out[19 + axis] = vel[axis, near_x - 2]
-        out[22] = (solid[near_x - 2] > 0).astype(F32)
 
 
 def adjoint_collide(u, is_solid, r, want):
@@ -483,7 +519,7 @@
     adj, pops, solid_h = in_hbm(adj_later), in_hbm(saved_pops), in_hbm(solid)
     scale = in_hbm(saved_scale.transpose(0, 2, 3, 4, 1).reshape(2, BX, 2 * BY, 19))
     block = pltpu.VMEM((24, 128), F32)
-    x_face = pltpu.VMEM((23, BY, BZ), F32)
+    x_face = pltpu.VMEM((24, BY, BZ), F32)
     y_face = pltpu.VMEM((Y_ROWS, BZ), F32)
     extended = pltpu.VMEM((19, EX, BY, BZ), F32)
     flow = pltpu.VMEM((3, BX, BY, BZ), F32)
@@ -500,8 +536,8 @@
             pltpu.SemaphoreType.DMA((3,)),
         ],
     )
-    left = in_vmem(shifted(high, "gx", 1))
-    right = in_vmem(shifted(low, "gx", -1))
+    below = in_vmem(shifted(high, "gy", 1))
+    above = in_vmem(shifted(low, "gy", -1))
 
     raw = pltpu.VMEM((19, BX, BY, BZ), jnp.bfloat16)
     table = pltpu.VMEM((BX, 2 * BY, 19), F32)
@@ -512,30 +548,33 @@
         (pops, scale, adj, solid_h),
         scratch=[raw, table, pltpu.SemaphoreType.DMA((5,))],
     )
-    down, same, up = call(regroup, (block,) * 3, [vmem] * 4, (left, mid, right, solid_v))
-    from_low = in_vmem(shifted(up, "gy", 1))
-    from_high = in_vmem(shifted(down, "gy", -1))
+    west, here, east = call(regroup, (block,) * 3, [vmem] * 4, (below, mid, above, solid_v))
     vel_early = call(
-        early_velocities, flow, [hbm, hbm, vmem], (pops, scale, same),
+        early_velocities, flow, [hbm, hbm, vmem], (pops, scale, here),
         scratch=[raw, table, pltpu.SemaphoreType.DMA((3,))],
     )
+    bf16 = jnp.bfloat16
     ext, to_left, to_right = call(
-        scatter,
+        own_seeds,
         (extended, x_face, x_face),
         [vmem] * 6,
-        (ext, from_low, same, from_high, vel_late, solid_v),
-        scratch=[
-            pltpu.VMEM((24, 384), F32), pltpu.VMEM((128, 384), jnp.bfloat16), pltpu.VMEM((BZ, 384), jnp.bfloat16),
-        ],
+        (ext, west, here, east, vel_late, solid_v),
+        scratch=[pltpu.VMEM((128, 128), bf16), pltpu.VMEM((BZ, 128), bf16)],
         aliases={0: 0},
     )
     from_left = in_vmem(shifted(to_right, "gx", 1))
     from_right = in_vmem(shifted(to_left, "gx", -1))
+    far_left = in_vmem(shifted(east, "gx", 2))
+    far_right = in_vmem(shifted(west, "gx", -2))
     ext, to_down, to_up = call(
         y_faces,
         (extended, y_face, y_face),
-        [vmem] * 5,
-        (ext, from_left, from_right, vel_late, solid_v),
+        [vmem] * 9,
+        (ext, from_left, from_right, far_left, far_right, west, east, vel_late, solid_v),
+        scratch=[
+            pltpu.VMEM((24, 256), F32), pltpu.VMEM((128, 256), bf16), pltpu.VMEM((BZ, 256), bf16),
+            pltpu.VMEM((608, 256), bf16),
+        ],
         aliases={0: 0},
     )
     from_down = in_vmem(shifted(to_up, "gy", 1))

time: 46.1 us -> 42.9 us (0.931)
  starting transfers between devices: 17.7 us -> 14.2 us
    ppermute x8, starting transfers between devices: 17.7 us -> 14.2 us  [shifted(): lax.ppermute(value, axis, [(i, (i + step) % count) for i in range(count)])]
  transfers between devices with their start and end apart: 8 -> 8, of which waited for: 5 -> 5; matrix products, arithmetic and copies ran while one was open for 0% -> 0% of each run, Pallas kernels for 12% -> 13%
where the time goes in v3:
time: 42.9 us; the launch traced here: 42.7 us
  waiting for transfers between devices  14.3 us (33%)
  starting transfers between devices  14.2 us (33%)
  Pallas kernels  13.5 us (31%)
  between operations  0.7 us (2%)
    ppermute x8, waiting for transfers between devices, shifted(): lax.ppermute(value, axis, [(i, (i + step) % count) for i in range(count)])  14.3 us
    ppermute x8, starting transfers between devices, shifted(): lax.ppermute(value, axis, [(i, (i + step) % count) for i in range(count)])  14.2 us
    pallas_call x7, Pallas kernels, call(): pl.pallas_call(body, out_shape=outs, in_specs=in_specs, out_specs=out_spe...  13.5 us
  transfers between devices with their start and end apart: 8, of which 5 were waited for; matrix products, arithmetic and copies ran while one was open for 0% of the time, Pallas kernels for 13%

profile of v3, /device:TPU:6, one launch (start us, length us, event | category | flops | bytes accessed | tf_op | source)
XLA Modules:
  0.0 42.7 jit_solution(17983041799674222423)
XLA Ops:
  0.6 1.3 %shard_map.87 = (f32[24,128]{1,0:T(8,128)S(1)}, f32[24,128]{1,0:T(8,128)S(1)}, f32[24,128]{1,0:T(8,128)S(1)}) custom-call(f32[19,128]{1,0:T(8,128)} %bitcast.8, s32[1,128]{1,0:T(1,128)} %bitcast.9, s32[1,128]{1,0:T(1,128)} %bitcast.10), custom_call_target="tpu_custom_call" | custom-call | tf_op jit(solution)/shard_map/pallas_call | solution.py:60
  2.0 1.6 %collective-permute-start = (f32[24,128]{1,0:T(8,128)S(1)}, f32[24,128]{1,0:T(8,128)S(1)}, u32[]{:S(2)}, u32[]{:S(2)}) collective-permute-start(f32[24,128]{1,0:T(8,128)S(1)} %get-tuple-element.18), channel_id=1, source_target_pairs={{0,1},{1,2},{2,3},{3,4},{4,5},{5,6},{6,7},{7,0},{8,9},{9,10},{10,1... | collective-permute-start | bytes 36872 | tf_op jit(solution)/shard_map/ppermute | solution.py:515
  3.5 0.5 %collective-permute-start.1 = (f32[24,128]{1,0:T(8,128)S(1)}, f32[24,128]{1,0:T(8,128)S(1)}, u32[]{:S(2)}, u32[]{:S(2)}) collective-permute-start(f32[24,128]{1,0:T(8,128)S(1)} %get-tuple-element.20), channel_id=1, source_target_pairs={{0,7},{1,0},{2,1},{3,2},{4,3},{5,4},{6,5},{7,6},{8,15},{9,8},{10,9... | collective-permute-start | bytes 36872 | tf_op jit(solution)/shard_map/ppermute | solution.py:515
  4.1 2.8 %shard_map.86 = (f32[3,8,16,256]{3,2,1,0:T(8,128)S(1)}, f32[19,12,16,256]{3,2,1,0:T(8,128)S(1)}, s32[8,16,256]{2,1,0:T(8,128)S(1)}) custom-call(bf16[2,19,8,16,256]{4,3,2,1,0:T(8,128)(2,1)} %pops.3, f32[2,8,32,19]{3,2,1,0:T(8,128)} %bitcast.6, f32[19,8,16,256]{3,2,1,0:T(8,128)} %adj.1, s32[8,16,256]{2,1,0:T(8,128)} %solid_in.1), custom_call_target="tpu_custom_call" | custom-call | tf_op jit(solution)/shard_map/pallas_call | solution.py:60
  6.9 0.0 collective-permute-done.below
  6.9 2.4 %collective-permute-done.1.above = f32[24,128]{1,0:T(8,128)S(1)} collective-permute-done((f32[24,128]{1,0:T(8,128)S(1)}, f32[24,128]{1,0:T(8,128)S(1)}, u32[]{:S(2)}, u32[]{:S(2)}) %collective-permute-start.1) | collective-permute-done | bytes 12320 | tf_op jit(solution)/shard_map/ppermute | solution.py:515
  9.3 0.1 shard_map.88
  9.4 0.8 %shard_map.89 = (f32[19,12,16,256]{3,2,1,0:T(8,128)S(1)}, f32[24,16,256]{2,1,0:T(8,128)S(1)}, f32[24,16,256]{2,1,0:T(8,128)S(1)}) custom-call(f32[19,12,16,256]{3,2,1,0:T(8,128)S(1)} %get-tuple-element.17.ext_in, f32[24,128]{1,0:T(8,128)S(1)} %get-tuple-element.22.west, f32[24,128]{1,0:T(8,128)S(1)} %get-tuple-element.23.here.after, ...), custom_call_target="tpu_custom_call", output_to_operand_aliasing={{0}: (0, {})} | custom-call | tf_op jit(solution)/shard_map/pallas_call | solution.py:60
  10.3 0.1 collective-permute-start.2
  10.4 6.3 %collective-permute-start.3 = (f32[24,16,256]{2,1,0:T(8,128)S(1)}, f32[24,16,256]{2,1,0:T(8,128)S(1)}, u32[]{:S(2)}, u32[]{:S(2)}) collective-permute-start(f32[24,16,256]{2,1,0:T(8,128)S(1)} %get-tuple-element.28), channel_id=1, source_target_pairs={{0,248},{8,0},{16,8},{24,16},{32,24},{40,32},{48,40},{56,48},{64,5... | collective-permute-start | bytes 1179656 | tf_op jit(solution)/shard_map/ppermute | solution.py:515
  16.6 3.6 %collective-permute-start.5 = (f32[24,128]{1,0:T(8,128)S(1)}, f32[24,128]{1,0:T(8,128)S(1)}, u32[]{:S(2)}, u32[]{:S(2)}) collective-permute-start(f32[24,128]{1,0:T(8,128)S(1)} %get-tuple-element.22.west), channel_id=1, source_target_pairs={{0,240},{8,248},{16,0},{24,8},{32,16},{40,24},{48,32},{56,40},{64,... | collective-permute-start | bytes 36872 | tf_op jit(solution)/shard_map/ppermute | solution.py:515
  20.3 0.0 collective-permute-start.4
  20.3 1.9 %collective-permute-done.5.far_right = f32[24,128]{1,0:T(8,128)S(1)} collective-permute-done((f32[24,128]{1,0:T(8,128)S(1)}, f32[24,128]{1,0:T(8,128)S(1)}, u32[]{:S(2)}, u32[]{:S(2)}) %collective-permute-start.5) | collective-permute-done | bytes 12320 | tf_op jit(solution)/shard_map/ppermute | solution.py:515
  22.2 5.4 %collective-permute-done.4.far_left = f32[24,128]{1,0:T(8,128)S(1)} collective-permute-done((f32[24,128]{1,0:T(8,128)S(1)}, f32[24,128]{1,0:T(8,128)S(1)}, u32[]{:S(2)}, u32[]{:S(2)}) %collective-permute-start.4) | collective-permute-done | bytes 12320 | tf_op jit(solution)/shard_map/ppermute | solution.py:515
  27.6 0.0 collective-permute-done.2.from_left
  27.6 0.0 collective-permute-done.3.from_right
  27.6 1.3 %shard_map.90 = (f32[19,12,16,256]{3,2,1,0:T(8,128)S(1)}, f32[280,256]{1,0:T(8,128)S(1)}, f32[280,256]{1,0:T(8,128)S(1)}) custom-call(f32[19,12,16,256]{3,2,1,0:T(8,128)S(1)} %get-tuple-element.26.ext_in, f32[24,16,256]{2,1,0:T(8,128)S(1)} %collective-permute-done.2.from_left, ...), custom_call_target="tpu_custom_call", output_to_operand_aliasing={{0}: (0, {})} | custom-call | tf_op jit(solution)/shard_map/pallas_call | solution.py:60
  28.9 0.7 %collective-permute-start.6 = (f32[280,256]{1,0:T(8,128)S(1)}, f32[280,256]{1,0:T(8,128)S(1)}, u32[]{:S(2)}, u32[]{:S(2)}) collective-permute-start(f32[280,256]{1,0:T(8,128)S(1)} %get-tuple-element.30.to_up), channel_id=1, source_target_pairs={{0,1},{1,2},{2,3},{3,4},{4,5},{5,6},{6,7},{7,0},{8,9},{9,10},{10,1... | collective-permute-start | bytes 860168 | tf_op jit(solution)/shard_map/ppermute | solution.py:515
  29.6 1.4 %collective-permute-start.7 = (f32[280,256]{1,0:T(8,128)S(1)}, f32[280,256]{1,0:T(8,128)S(1)}, u32[]{:S(2)}, u32[]{:S(2)}) collective-permute-start(f32[280,256]{1,0:T(8,128)S(1)} %get-tuple-element.31.to_down), channel_id=1, source_target_pairs={{0,7},{1,0},{2,1},{3,2},{4,3},{5,4},{6,5},{7,6},{8,15},{9,8},{10,9... | collective-permute-start | bytes 860168 | tf_op jit(solution)/shard_map/ppermute | solution.py:515
  31.0 2.8 %shard_map.91.vel_early = f32[3,8,16,256]{3,2,1,0:T(8,128)S(1)} custom-call(bf16[2,19,8,16,256]{4,3,2,1,0:T(8,128)(2,1)} %pops.3, f32[2,8,32,19]{3,2,1,0:T(8,128)} %bitcast.7, f32[24,128]{1,0:T(8,128)S(1)} %get-tuple-element.23.here.after), custom_call_target="tpu_custom_call" | custom-call | tf_op jit(solution)/shard_map/pallas_call | solution.py:60
  33.8 1.8 %collective-permute-done.6.from_down = f32[280,256]{1,0:T(8,128)S(1)} collective-permute-done((f32[280,256]{1,0:T(8,128)S(1)}, f32[280,256]{1,0:T(8,128)S(1)}, u32[]{:S(2)}, u32[]{:S(2)}) %collective-permute-start.6) | collective-permute-done | bytes 286752 | tf_op jit(solution)/shard_map/ppermute | solution.py:515
  35.6 2.7 %collective-permute-done.7.from_up = f32[280,256]{1,0:T(8,128)S(1)} collective-permute-done((f32[280,256]{1,0:T(8,128)S(1)}, f32[280,256]{1,0:T(8,128)S(1)}, u32[]{:S(2)}, u32[]{:S(2)}) %collective-permute-start.7) | collective-permute-done | bytes 286752 | tf_op jit(solution)/shard_map/ppermute | solution.py:515
  38.3 4.4 %shard_map.92 = (f32[19,8,16,256]{3,2,1,0:T(8,128)}, f32[19,8,16,256]{3,2,1,0:T(8,128)}) custom-call(f32[19,12,16,256]{3,2,1,0:T(8,128)S(1)} %get-tuple-element.29.ext, f32[24,16,256]{2,1,0:T(8,128)S(1)} %collective-permute-done.2.from_left, f32[24,16,256]{2,1,0:T(8,128)S(1)} %collective-permute-done.3.from_right, ...), custom_call_target="tpu_custom_call" | custom-call | tf_op jit(solution)/shard_map/pallas_call | solution.py:60
Async XLA Ops:
  2.0 4.9 %collective-permute-start = (f32[24,128]{1,0:T(8,128)S(1)}, f32[24,128]{1,0:T(8,128)S(1)}, u32[]{:S(2)}, u32[]{:S(2)}) collective-permute-start(f32[24,128]{1,0:T(8,128)S(1)} %get-tuple-element.18), channel_id=1, source_target_pairs={{0,1},{1,2},{2,3},{3,4},{4,5},{5,6},{6,7},{7,0},{8,9},{9,10},{10,1... | collective-permute-start | bytes 36872 | tf_op jit(solution)/shard_map/ppermute | solution.py:515
  3.5 5.8 %collective-permute-start.1 = (f32[24,128]{1,0:T(8,128)S(1)}, f32[24,128]{1,0:T(8,128)S(1)}, u32[]{:S(2)}, u32[]{:S(2)}) collective-permute-start(f32[24,128]{1,0:T(8,128)S(1)} %get-tuple-element.20), channel_id=1, source_target_pairs={{0,7},{1,0},{2,1},{3,2},{4,3},{5,4},{6,5},{7,6},{8,15},{9,8},{10,9... | collective-permute-start | bytes 36872 | tf_op jit(solution)/shard_map/ppermute | solution.py:515
  10.3 17.3 %collective-permute-start.2 = (f32[24,16,256]{2,1,0:T(8,128)S(1)}, f32[24,16,256]{2,1,0:T(8,128)S(1)}, u32[]{:S(2)}, u32[]{:S(2)}) collective-permute-start(f32[24,16,256]{2,1,0:T(8,128)S(1)} %get-tuple-element.27), channel_id=1, source_target_pairs={{0,8},{8,16},{16,24},{24,32},{32,40},{40,48},{48,56},{56,64},{64,7... | collective-permute-start | bytes 1179656 | tf_op jit(solution)/shard_map/ppermute | solution.py:515
  10.4 17.2 %collective-permute-start.3 = (f32[24,16,256]{2,1,0:T(8,128)S(1)}, f32[24,16,256]{2,1,0:T(8,128)S(1)}, u32[]{:S(2)}, u32[]{:S(2)}) collective-permute-start(f32[24,16,256]{2,1,0:T(8,128)S(1)} %get-tuple-element.28), channel_id=1, source_target_pairs={{0,248},{8,0},{16,8},{24,16},{32,24},{40,32},{48,40},{56,48},{64,5... | collective-permute-start | bytes 1179656 | tf_op jit(solution)/shard_map/ppermute | solution.py:515
  16.6 5.6 %collective-permute-start.5 = (f32[24,128]{1,0:T(8,128)S(1)}, f32[24,128]{1,0:T(8,128)S(1)}, u32[]{:S(2)}, u32[]{:S(2)}) collective-permute-start(f32[24,128]{1,0:T(8,128)S(1)} %get-tuple-element.22.west), channel_id=1, source_target_pairs={{0,240},{8,248},{16,0},{24,8},{32,16},{40,24},{48,32},{56,40},{64,... | collective-permute-start | bytes 36872 | tf_op jit(solution)/shard_map/ppermute | solution.py:515
  20.3 7.3 %collective-permute-start.4 = (f32[24,128]{1,0:T(8,128)S(1)}, f32[24,128]{1,0:T(8,128)S(1)}, u32[]{:S(2)}, u32[]{:S(2)}) collective-permute-start(f32[24,128]{1,0:T(8,128)S(1)} %get-tuple-element.24.east), channel_id=1, source_target_pairs={{0,16},{8,24},{16,32},{24,40},{32,48},{40,56},{48,64},{56,72},{64,... | collective-permute-start | bytes 36872 | tf_op jit(solution)/shard_map/ppermute | solution.py:515
  28.9 6.7 %collective-permute-start.6 = (f32[280,256]{1,0:T(8,128)S(1)}, f32[280,256]{1,0:T(8,128)S(1)}, u32[]{:S(2)}, u32[]{:S(2)}) collective-permute-start(f32[280,256]{1,0:T(8,128)S(1)} %get-tuple-element.30.to_up), channel_id=1, source_target_pairs={{0,1},{1,2},{2,3},{3,4},{4,5},{5,6},{6,7},{7,0},{8,9},{9,10},{10,1... | collective-permute-start | bytes 860168 | tf_op jit(solution)/shard_map/ppermute | solution.py:515
  29.6 8.7 %collective-permute-start.7 = (f32[280,256]{1,0:T(8,128)S(1)}, f32[280,256]{1,0:T(8,128)S(1)}, u32[]{:S(2)}, u32[]{:S(2)}) collective-permute-start(f32[280,256]{1,0:T(8,128)S(1)} %get-tuple-element.31.to_down), channel_id=1, source_target_pairs={{0,7},{1,0},{2,1},{3,2},{4,3},{5,4},{6,5},{7,6},{8,15},{9,8},{10,9... | collective-permute-start | bytes 860168 | tf_op jit(solution)/shard_map/ppermute | solution.py:515

commit v4 on v3

--- a/solution.py
+++ b/solution.py
@@ -177,14 +177,6 @@
     next(work)
 
 
-def held(i, x):
-    if x in (0, EX - 1):
-        return VEL[i][0] == (-1 if x == 0 else 1)
-    if x in (1, EX - 2):
-        return VEL[i][0] in (0, -1 if x == 1 else 1)
-    return True
-
-
 def regroup(below, own, above, after, west, here, east):
     del after
     gy = lax.axis_index("gy")
@@ -201,11 +193,19 @@
         )
 
 
-Y_ROWS = 23 * EX + 4
-
-
-def put(entry, x):
-    return slice(EX * entry + x, EX * entry + x + 1)
+Y_LEAD = 8
+Y_HELD = BX + 2
+Y_ROWS = Y_LEAD + 23 * Y_HELD + 10
+
+
+def put(n, x, shift):
+    row = Y_LEAD + Y_HELD * n + x - 1 - shift
+    return slice(row, row + 1)
+
+
+def entry(face, n, shift):
+    first = Y_LEAD + Y_HELD * n - 1 - shift
+    return face[first : first + 16, :]
 
 
 def halves(v):
@@ -294,19 +294,20 @@
         )
     for sign, out, near_y, far_y in ((1, to_down, 0, 1), (-1, to_up, BY - 1, BY - 2)):
         near, far = face_rows(1, sign)
-        out[...] = jnp.zeros((Y_ROWS, BZ), F32)
+        out[0:Y_LEAD, :] = jnp.zeros((Y_LEAD, BZ), F32)
+        out[Y_ROWS - 10 : Y_ROWS, :] = jnp.zeros((10, BZ), F32)
         for base, pops, y in ((0, near, near_y), (14, far, far_y)):
             for slot, i in enumerate(pops):
-                for x in range(EX):
-                    if held(i, x):
-                        out[put(base + slot, x), :] = ext[i, x, y : y + 1, :]
+                shift = VEL[i][0]
+                for x in range(1 + shift, EX - 1 + shift):
+                    out[put(base + slot, x, shift), :] = ext[i, x, y : y + 1, :]
         for row in range(19, 23):
-            out[put(row, 1), :] = from_left[row, near_y : near_y + 1, :]
-            out[put(row, 10), :] = from_right[row, near_y : near_y + 1, :]
+            out[put(row, 1, 0), :] = from_left[row, near_y : near_y + 1, :]
+            out[put(row, EX - 2, 0), :] = from_right[row, near_y : near_y + 1, :]
         for x in range(BX):
             for axis in range(3):
-                out[put(19 + axis, x + 2), :] = vel[axis, x, near_y : near_y + 1, :]
-            out[put(22, x + 2), :] = (solid[x, near_y : near_y + 1, :] > 0).astype(F32)
+                out[put(19 + axis, x + 2, 0), :] = vel[axis, x, near_y : near_y + 1, :]
+            out[put(22, x + 2, 0), :] = (solid[x, near_y : near_y + 1, :] > 0).astype(F32)
 
 
 def adjoint_collide(u, is_solid, r, want):
@@ -371,17 +372,21 @@
     return jnp.where(lane == 0, 0.0, pltpu.roll(v, 1, 1))
 
 
-def read_plane(field, low_face, high_face, x, i, low_slot, high_slot):
+def read_plane(field, x, i, low_face=None, high_face=None):
     cx, cy, cz = VEL[i]
     v = field[i, x + cx]
     if cy:
         row = iota(v.shape, 0)
         if cy > 0:
-            edge = high_face[high_slot[i], pl.ds(x + cx, 1), :]
-            v = jnp.where(row == BY - 1, jnp.broadcast_to(edge, v.shape), pltpu.roll(v, BY - 1, 0))
+            v = pltpu.roll(v, BY - 1, 0)
+            if high_face is not None:
+                edge = high_face[FAR_UP[i], pl.ds(x + cx, 1), :]
+                v = jnp.where(row == BY - 1, jnp.broadcast_to(edge, v.shape), v)
         else:
-            edge = low_face[low_slot[i], pl.ds(x + cx, 1), :]
-            v = jnp.where(row == 0, jnp.broadcast_to(edge, v.shape), pltpu.roll(v, 1, 0))
+            v = pltpu.roll(v, 1, 0)
+            if low_face is not None:
+                edge = low_face[FAR_DOWN[i], pl.ds(x + cx, 1), :]
+                v = jnp.where(row == 0, jnp.broadcast_to(edge, v.shape), v)
     return shift_z(v, cz)
 
 
@@ -396,29 +401,17 @@
                 store(i, rows, lanes, out[i])
 
 
-def entry(face, n):
-    return face[EX * n : EX * n + 16, :]
-
-
-def two_steps(
-    ext, from_left, from_right, from_down, from_up, to_down, to_up, vel_late, vel_early, solid,
-    initial, middle,
-    mid_ext, first, low_near, high_near, low_face, high_face, reads, mid_sems, first_sems,
-):
-    gx, gy = lax.axis_index("gx"), lax.axis_index("gy")
-    in_left, in_right = gx > 0, gx < lax.axis_size("gx") - 1
-    in_down, in_up = gy > 0, gy < lax.axis_size("gy") - 1
-
-    for n in range(14):
-        low_near[n] = jnp.where(in_down, entry(from_down, n), 0.0)
-        high_near[n] = jnp.where(in_up, entry(from_up, n), 0.0)
-
-    for x, ref, ok, sign in ((1, from_left, in_left, -1), (EX - 2, from_right, in_right, 1)):
+def late_planes(ext, from_left, from_right, vel, solid, mid, reads):
+    gx = lax.axis_index("gx")
+    for x, ref, ok, sign in (
+        (1, from_left, gx > 0, -1),
+        (EX - 2, from_right, gx < lax.axis_size("gx") - 1, 1),
+    ):
         for i in range(19):
-            reads[i] = read_plane(ext, low_near, high_near, x, i, NEAR_DOWN, NEAR_UP)
+            reads[i] = read_plane(ext, x, i)
 
         def keep(i, rows, lanes, value, x=x, ok=ok):
-            mid_ext[i, x, rows, lanes] = jnp.where(ok, value, 0.0)
+            mid[i, x, rows, lanes] = jnp.where(ok, value, 0.0)
 
         collide_block(
             reads,
@@ -428,71 +421,103 @@
             keep,
         )
 
-    for ref, mine, mine_slot, near, far, sign, ok, out in (
-        (from_down, to_down, NEAR_UP, NEAR_DOWN, FAR_DOWN, -1, in_down, low_face),
-        (from_up, to_up, NEAR_DOWN, NEAR_UP, FAR_UP, 1, in_up, high_face),
-    ):
+    def plane(x, carry):
         for i in range(19):
-            cx, cy, cz = VEL[i]
-            if cy == 0:
-                v = entry(ref, near[i])
-            elif cy == sign:
-                v = entry(ref, 14 + far[i])
-            else:
-                v = entry(mine, mine_slot[i])
-            if cx:
-                v = pltpu.roll(v, (-cx) % 16, 0)
-            reads[i] = shift_z(v, cz)
-        row = iota((8, 128), 0)
-
-        def keep_row(i, rows, lanes, value, out=out, far=far, ok=ok):
-            x = row + rows.start
-            good = ok & ((x > 1) | in_left) & ((x < EX - 2) | in_right)
-            out[far[i], rows, lanes] = jnp.where(good, value, 0.0)
+            reads[i] = read_plane(ext, x + 2, i)
+
+        def keep(i, rows, lanes, value):
+            mid[i, x + 2, rows, lanes] = value
 
         collide_block(
             reads,
-            lambda axis, rows, lanes, ref=ref: entry(ref, 19 + axis)[rows, lanes],
-            lambda rows, lanes, ref=ref: entry(ref, 22)[rows, lanes] > 0.0,
-            face_rows(1, sign)[1],
-            keep_row,
-        )
-
-    def mid_copy(x):
-        return pltpu.make_async_copy(mid_ext.at[:, pl.ds(x + 2, 1)], middle.at[:, pl.ds(x, 1)], mid_sems.at[x])
-
-    def first_copy(x):
-        return pltpu.make_async_copy(first.at[:, pl.ds(x, 1)], initial.at[:, pl.ds(x, 1)], first_sems.at[x])
-
-    def mid_plane(x, carry):
-        for i in range(19):
-            reads[i] = read_plane(ext, low_near, high_near, x + 2, i, NEAR_DOWN, NEAR_UP)
-
-        def keep(i, rows, lanes, value):
-            mid_ext[i, x + 2, rows, lanes] = value
-
-        collide_block(
-            reads,
-            lambda axis, rows, lanes: vel_late[axis, x, rows, lanes],
+            lambda axis, rows, lanes: vel[axis, x, rows, lanes],
             lambda rows, lanes: solid[x, rows, lanes] > 0,
             ALL,
             keep,
         )
-        mid_copy(x).start()
         return carry
 
-    lax.fori_loop(0, BX, mid_plane, 0)
-
-    def first_plane(x, carry):
+    lax.fori_loop(0, BX, plane, 0)
+
+
+def finish_steps(
+    mid_in, from_down, from_up, to_down, to_up, vel, solid,
+    initial, middle, mid,
+    first, low_face, high_face, reads, mid_sem, first_sems,
+):
+    del mid_in
+    gx, gy = lax.axis_index("gx"), lax.axis_index("gy")
+    in_left, in_right = gx > 0, gx < lax.axis_size("gx") - 1
+    in_down, in_up = gy > 0, gy < lax.axis_size("gy") - 1
+    row = iota((8, 128), 0)
+
+    for ref, mine, near, far, mine_near, mine_far, sign, ok, out, y in (
+        (from_down, to_down, NEAR_DOWN, FAR_DOWN, NEAR_UP, FAR_UP, -1, in_down, low_face, 0),
+        (from_up, to_up, NEAR_UP, FAR_UP, NEAR_DOWN, FAR_DOWN, 1, in_up, high_face, BY - 1),
+    ):
+        for inside in (False, True):
+            for i in range(19):
+                cx, cy, cz = VEL[i]
+                if inside:
+                    if cy == 0:
+                        v = entry(mine, mine_near[i], cx)
+                    elif cy == sign:
+                        v = jnp.where(ok, entry(ref, near[i], cx), 0.0)
+                    else:
+                        v = entry(mine, 14 + mine_far[i], cx)
+                elif cy == 0:
+                    v = entry(ref, near[i], cx)
+                elif cy == sign:
+                    v = entry(ref, 14 + far[i], cx)
+                else:
+                    v = entry(mine, mine_near[i], cx)
+                if cx:
+                    v = pltpu.roll(v, (-cx) % 16, 0)
+                reads[i] = shift_z(v, cz)
+
+            def keep_face(i, rows, lanes, value, out=out, far=far, ok=ok):
+                x = row + rows.start
+                good = ok & ((x > 1) | in_left) & ((x < EX - 2) | in_right)
+                out[far[i], rows, lanes] = jnp.where(good, value, 0.0)
+
+            def keep_row(i, rows, lanes, value, y=y):
+                for x in range(max(1, rows.start), min(EX - 1, rows.stop)):
+                    one = value[x - rows.start : x - rows.start + 1, :]
+                    if x == 1:
+                        if VEL[i][0] != -1:
+                            continue
+                        one = jnp.where(in_left, one, 0.0)
+                    elif x == EX - 2:
+                        if VEL[i][0] != 1:
+                            continue
+                        one = jnp.where(in_right, one, 0.0)
+                    mid[i, x, y : y + 1, lanes] = one
+
+            source = mine if inside else ref
+            collide_block(
+                reads,
+                lambda axis, rows, lanes, source=source: entry(source, 19 + axis, 0)[rows, lanes],
+                lambda rows, lanes, source=source: entry(source, 22, 0)[rows, lanes] > 0.0,
+                ALL if inside else face_rows(1, sign)[1],
+                keep_row if inside else keep_face,
+            )
+
+    mid_copy = pltpu.make_async_copy(mid.at[:, pl.ds(2, BX)], middle, mid_sem)
+    mid_copy.start()
+
+    def first_copy(x):
+        return pltpu.make_async_copy(first.at[:, pl.ds(x, 1)], initial.at[:, pl.ds(x, 1)], first_sems.at[x])
+
+    def plane(x, carry):
         for i in range(19):
-            reads[i] = read_plane(mid_ext, low_face, high_face, x + 2, i, FAR_DOWN, FAR_UP)
+            reads[i] = read_plane(mid, x + 2, i, low_face, high_face)
 
         def keep(i, rows, lanes, value):
             first[i, x, rows, lanes] = value
 
         collide_block(
             reads,
-            lambda axis, rows, lanes: vel_early[axis, x, rows, lanes],
+            lambda axis, rows, lanes: vel[axis, x, rows, lanes],
             lambda rows, lanes: solid[x, rows, lanes] > 0,
             ALL,
             keep,
@@ -500,14 +525,14 @@
         first_copy(x).start()
         return carry
 
-    lax.fori_loop(0, BX, first_plane, 0)
-
-    def finish(x, carry):
-        mid_copy(x).wait()
+    lax.fori_loop(0, BX, plane, 0)
+    mid_copy.wait()
+
+    def drain(x, carry):
         first_copy(x).wait()
         return carry
 
-    lax.fori_loop(0, BX, finish, 0)
+    lax.fori_loop(0, BX, drain, 0)
 
 
 def shifted(value, axis, step):
@@ -579,24 +604,27 @@
     )
     from_down = in_vmem(shifted(to_up, "gy", 1))
     from_up = in_vmem(shifted(to_down, "gy", -1))
+    reads = pltpu.VMEM((19, BY, BZ), F32)
+    mid = call(
+        late_planes, extended, [vmem] * 5, (ext, from_left, from_right, vel_late, solid_v), scratch=[reads]
+    )
     field = jax.ShapeDtypeStruct((19, BX, BY, BZ), F32)
-    return call(
-        two_steps,
-        (field, field),
-        [vmem] * 10,
-        (ext, from_left, from_right, from_down, from_up, to_down, to_up, vel_late, vel_early, solid_v),
+    initial, middle, _ = call(
+        finish_steps,
+        (field, field, extended),
+        [vmem] * 7,
+        (mid, from_down, from_up, to_down, to_up, vel_early, solid_v),
         scratch=[
-            pltpu.VMEM((19, EX, BY, BZ), F32),
             pltpu.VMEM((19, BX, BY, BZ), F32),
-            pltpu.VMEM((14, 16, BZ), F32),
-            pltpu.VMEM((14, 16, BZ), F32),
             pltpu.VMEM((5, 16, BZ), F32),
             pltpu.VMEM((5, 16, BZ), F32),
-            pltpu.VMEM((19, BY, BZ), F32),
-            pltpu.SemaphoreType.DMA((BX,)),
+            reads,
+            pltpu.SemaphoreType.DMA(()),
             pltpu.SemaphoreType.DMA((BX,)),
         ],
-    )
+        aliases={0: 2},
+    )
+    return initial, middle
 
 
 def solution(mesh):

time: 42.9 us -> 41.6 us (0.970)
  waiting for transfers between devices: 14.3 us -> 12.2 us
  Pallas kernels: 13.5 us -> 14.3 us
    ppermute x8, waiting for transfers between devices: 14.3 us -> 12.2 us  [shifted(): lax.ppermute(value, axis, [(i, (i + step) % count) for i in range(count)])]
    pallas_call x7 -> x8, Pallas kernels: 13.5 us -> 14.3 us  [call(): pl.pallas_call(body, out_shape=outs, in_specs=in_specs, out_specs=out_spe...]
  transfers between devices with their start and end apart: 8 -> 8, of which waited for: 5 -> 4; matrix products, arithmetic and copies ran while one was open for 0% -> 0% of each run, Pallas kernels for 13% -> 18%
where the time goes in v4:
time: 41.6 us; the launch traced here: 41.5 us
  Pallas kernels  14.3 us (34%)
  starting transfers between devices  14.2 us (34%)
  waiting for transfers between devices  12.2 us (29%)
  between operations  0.71 us (2%)
    pallas_call x8, Pallas kernels, call(): pl.pallas_call(body, out_shape=outs, in_specs=in_specs, out_specs=out_spe...  14.3 us
    ppermute x8, starting transfers between devices, shifted(): lax.ppermute(value, axis, [(i, (i + step) % count) for i in range(count)])  14.2 us
    ppermute x8, waiting for transfers between devices, shifted(): lax.ppermute(value, axis, [(i, (i + step) % count) for i in range(count)])  12.2 us
  transfers between devices with their start and end apart: 8, of which 4 were waited for; matrix products, arithmetic and copies ran while one was open for 0% of the time, Pallas kernels for 18%

profile of v4, /device:TPU:6, one launch (start us, length us, event | category | flops | bytes accessed | tf_op | source)
XLA Modules:
  0.0 41.5 jit_solution(9613121734491254724)
XLA Ops:
  0.6 1.3 %shard_map.87 = (f32[24,128]{1,0:T(8,128)S(1)}, f32[24,128]{1,0:T(8,128)S(1)}, f32[24,128]{1,0:T(8,128)S(1)}) custom-call(f32[19,128]{1,0:T(8,128)} %bitcast.8, s32[1,128]{1,0:T(1,128)} %bitcast.9, s32[1,128]{1,0:T(1,128)} %bitcast.10), custom_call_target="tpu_custom_call" | custom-call | tf_op jit(solution)/shard_map/pallas_call | solution.py:60
  2.0 1.6 %collective-permute-start = (f32[24,128]{1,0:T(8,128)S(1)}, f32[24,128]{1,0:T(8,128)S(1)}, u32[]{:S(2)}, u32[]{:S(2)}) collective-permute-start(f32[24,128]{1,0:T(8,128)S(1)} %get-tuple-element.20), channel_id=1, source_target_pairs={{0,1},{1,2},{2,3},{3,4},{4,5},{5,6},{6,7},{7,0},{8,9},{9,10},{10,1... | collective-permute-start | bytes 36872 | tf_op jit(solution)/shard_map/ppermute | solution.py:540
  3.5 0.5 %collective-permute-start.1 = (f32[24,128]{1,0:T(8,128)S(1)}, f32[24,128]{1,0:T(8,128)S(1)}, u32[]{:S(2)}, u32[]{:S(2)}) collective-permute-start(f32[24,128]{1,0:T(8,128)S(1)} %get-tuple-element.22), channel_id=1, source_target_pairs={{0,7},{1,0},{2,1},{3,2},{4,3},{5,4},{6,5},{7,6},{8,15},{9,8},{10,9... | collective-permute-start | bytes 36872 | tf_op jit(solution)/shard_map/ppermute | solution.py:540
  4.1 2.8 %shard_map.86 = (f32[3,8,16,256]{3,2,1,0:T(8,128)S(1)}, f32[19,12,16,256]{3,2,1,0:T(8,128)S(1)}, s32[8,16,256]{2,1,0:T(8,128)S(1)}) custom-call(bf16[2,19,8,16,256]{4,3,2,1,0:T(8,128)(2,1)} %pops.3, f32[2,8,32,19]{3,2,1,0:T(8,128)} %bitcast.6, f32[19,8,16,256]{3,2,1,0:T(8,128)} %adj.1, s32[8,16,256]{2,1,0:T(8,128)} %solid_in.1), custom_call_target="tpu_custom_call" | custom-call | tf_op jit(solution)/shard_map/pallas_call | solution.py:60
  6.9 0.0 collective-permute-done.below
  6.9 2.4 %collective-permute-done.1.above = f32[24,128]{1,0:T(8,128)S(1)} collective-permute-done((f32[24,128]{1,0:T(8,128)S(1)}, f32[24,128]{1,0:T(8,128)S(1)}, u32[]{:S(2)}, u32[]{:S(2)}) %collective-permute-start.1) | collective-permute-done | bytes 12320 | tf_op jit(solution)/shard_map/ppermute | solution.py:540
  9.3 0.1 shard_map.88
  9.4 0.8 %shard_map.89 = (f32[19,12,16,256]{3,2,1,0:T(8,128)S(1)}, f32[24,16,256]{2,1,0:T(8,128)S(1)}, f32[24,16,256]{2,1,0:T(8,128)S(1)}) custom-call(f32[19,12,16,256]{3,2,1,0:T(8,128)S(1)} %get-tuple-element.19.ext_in, f32[24,128]{1,0:T(8,128)S(1)} %get-tuple-element.24.west, f32[24,128]{1,0:T(8,128)S(1)} %get-tuple-element.25.here.after, ...), custom_call_target="tpu_custom_call", output_to_operand_aliasing={{0}: (0, {})} | custom-call | tf_op jit(solution)/shard_map/pallas_call | solution.py:60
  10.3 0.1 collective-permute-start.2
  10.4 6.3 %collective-permute-start.3 = (f32[24,16,256]{2,1,0:T(8,128)S(1)}, f32[24,16,256]{2,1,0:T(8,128)S(1)}, u32[]{:S(2)}, u32[]{:S(2)}) collective-permute-start(f32[24,16,256]{2,1,0:T(8,128)S(1)} %get-tuple-element.30), channel_id=1, source_target_pairs={{0,248},{8,0},{16,8},{24,16},{32,24},{40,32},{48,40},{56,48},{64,5... | collective-permute-start | bytes 1179656 | tf_op jit(solution)/shard_map/ppermute | solution.py:540
  16.6 3.6 %collective-permute-start.5 = (f32[24,128]{1,0:T(8,128)S(1)}, f32[24,128]{1,0:T(8,128)S(1)}, u32[]{:S(2)}, u32[]{:S(2)}) collective-permute-start(f32[24,128]{1,0:T(8,128)S(1)} %get-tuple-element.24.west), channel_id=1, source_target_pairs={{0,240},{8,248},{16,0},{24,8},{32,16},{40,24},{48,32},{56,40},{64,... | collective-permute-start | bytes 36872 | tf_op jit(solution)/shard_map/ppermute | solution.py:540
  20.3 0.0 collective-permute-start.4
  20.3 1.9 %collective-permute-done.5.far_right = f32[24,128]{1,0:T(8,128)S(1)} collective-permute-done((f32[24,128]{1,0:T(8,128)S(1)}, f32[24,128]{1,0:T(8,128)S(1)}, u32[]{:S(2)}, u32[]{:S(2)}) %collective-permute-start.5) | collective-permute-done | bytes 12320 | tf_op jit(solution)/shard_map/ppermute | solution.py:540
  22.2 5.4 %collective-permute-done.4.far_left = f32[24,128]{1,0:T(8,128)S(1)} collective-permute-done((f32[24,128]{1,0:T(8,128)S(1)}, f32[24,128]{1,0:T(8,128)S(1)}, u32[]{:S(2)}, u32[]{:S(2)}) %collective-permute-start.4) | collective-permute-done | bytes 12320 | tf_op jit(solution)/shard_map/ppermute | solution.py:540
  27.6 0.0 collective-permute-done.2.from_left
  27.6 0.0 collective-permute-done.3.from_right
  27.6 1.2 %shard_map.90 = (f32[19,12,16,256]{3,2,1,0:T(8,128)S(1)}, f32[248,256]{1,0:T(8,128)S(1)}, f32[248,256]{1,0:T(8,128)S(1)}) custom-call(f32[19,12,16,256]{3,2,1,0:T(8,128)S(1)} %get-tuple-element.28.ext_in, f32[24,16,256]{2,1,0:T(8,128)S(1)} %collective-permute-done.2.from_left, ...), custom_call_target="tpu_custom_call", output_to_operand_aliasing={{0}: (0, {})} | custom-call | tf_op jit(solution)/shard_map/pallas_call | solution.py:60
  28.8 0.7 %collective-permute-start.6 = (f32[248,256]{1,0:T(8,128)S(1)}, f32[248,256]{1,0:T(8,128)S(1)}, u32[]{:S(2)}, u32[]{:S(2)}) collective-permute-start(f32[248,256]{1,0:T(8,128)S(1)} %get-tuple-element.32.to_up), channel_id=1, source_target_pairs={{0,1},{1,2},{2,3},{3,4},{4,5},{5,6},{6,7},{7,0},{8,9},{9,10},{10,1... | collective-permute-start | bytes 761864 | tf_op jit(solution)/shard_map/ppermute | solution.py:540
  29.5 1.4 %collective-permute-start.7 = (f32[248,256]{1,0:T(8,128)S(1)}, f32[248,256]{1,0:T(8,128)S(1)}, u32[]{:S(2)}, u32[]{:S(2)}) collective-permute-start(f32[248,256]{1,0:T(8,128)S(1)} %get-tuple-element.33.to_down), channel_id=1, source_target_pairs={{0,7},{1,0},{2,1},{3,2},{4,3},{5,4},{6,5},{7,6},{8,15},{9,8},{10,9... | collective-permute-start | bytes 761864 | tf_op jit(solution)/shard_map/ppermute | solution.py:540
  30.9 2.8 %shard_map.92.vel = f32[3,8,16,256]{3,2,1,0:T(8,128)S(1)} custom-call(bf16[2,19,8,16,256]{4,3,2,1,0:T(8,128)(2,1)} %pops.3, f32[2,8,32,19]{3,2,1,0:T(8,128)} %bitcast.7, f32[24,128]{1,0:T(8,128)S(1)} %get-tuple-element.25.here.after), custom_call_target="tpu_custom_call" | custom-call | tf_op jit(solution)/shard_map/pallas_call | solution.py:60
  33.7 1.7 %shard_map.91.mid_in = f32[19,12,16,256]{3,2,1,0:T(8,128)S(1)} custom-call(f32[19,12,16,256]{3,2,1,0:T(8,128)S(1)} %get-tuple-element.31.ext, f32[24,16,256]{2,1,0:T(8,128)S(1)} %collective-permute-done.2.from_left, f32[24,16,256]{2,1,0:T(8,128)S(1)} %collective-permute-done.3.from_right, f32[3,8,16,256]{3,2,1,0:T(8,128)S(1)} %get-tuple-element.27.vel, ...), custom_call_target="tpu_custom_call" | custom-call | tf_op jit(solution)/shard_map/pallas_call | solution.py:60
  35.4 0.0 collective-permute-done.6.from_down
  35.4 2.5 %collective-permute-done.7.from_up = f32[248,256]{1,0:T(8,128)S(1)} collective-permute-done((f32[248,256]{1,0:T(8,128)S(1)}, f32[248,256]{1,0:T(8,128)S(1)}, u32[]{:S(2)}, u32[]{:S(2)}) %collective-permute-start.7) | collective-permute-done | bytes 253984 | tf_op jit(solution)/shard_map/ppermute | solution.py:540
  37.9 3.6 %shard_map.93 = (f32[19,8,16,256]{3,2,1,0:T(8,128)}, f32[19,8,16,256]{3,2,1,0:T(8,128)}, f32[19,12,16,256]{3,2,1,0:T(8,128)S(1)}) custom-call(f32[19,12,16,256]{3,2,1,0:T(8,128)S(1)} %shard_map.91.mid_in, f32[248,256]{1,0:T(8,128)S(1)} %collective-permute-done.6.from_down, ...), custom_call_target="tpu_custom_call", output_to_operand_aliasing={{2}: (0, {})} | custom-call | tf_op jit(solution)/shard_map/pallas_call | solution.py:60
Async XLA Ops:
  2.0 4.9 %collective-permute-start = (f32[24,128]{1,0:T(8,128)S(1)}, f32[24,128]{1,0:T(8,128)S(1)}, u32[]{:S(2)}, u32[]{:S(2)}) collective-permute-start(f32[24,128]{1,0:T(8,128)S(1)} %get-tuple-element.20), channel_id=1, source_target_pairs={{0,1},{1,2},{2,3},{3,4},{4,5},{5,6},{6,7},{7,0},{8,9},{9,10},{10,1... | collective-permute-start | bytes 36872 | tf_op jit(solution)/shard_map/ppermute | solution.py:540
  3.5 5.8 %collective-permute-start.1 = (f32[24,128]{1,0:T(8,128)S(1)}, f32[24,128]{1,0:T(8,128)S(1)}, u32[]{:S(2)}, u32[]{:S(2)}) collective-permute-start(f32[24,128]{1,0:T(8,128)S(1)} %get-tuple-element.22), channel_id=1, source_target_pairs={{0,7},{1,0},{2,1},{3,2},{4,3},{5,4},{6,5},{7,6},{8,15},{9,8},{10,9... | collective-permute-start | bytes 36872 | tf_op jit(solution)/shard_map/ppermute | solution.py:540
  10.3 17.3 %collective-permute-start.2 = (f32[24,16,256]{2,1,0:T(8,128)S(1)}, f32[24,16,256]{2,1,0:T(8,128)S(1)}, u32[]{:S(2)}, u32[]{:S(2)}) collective-permute-start(f32[24,16,256]{2,1,0:T(8,128)S(1)} %get-tuple-element.29), channel_id=1, source_target_pairs={{0,8},{8,16},{16,24},{24,32},{32,40},{40,48},{48,56},{56,64},{64,7... | collective-permute-start | bytes 1179656 | tf_op jit(solution)/shard_map/ppermute | solution.py:540
  10.4 17.2 %collective-permute-start.3 = (f32[24,16,256]{2,1,0:T(8,128)S(1)}, f32[24,16,256]{2,1,0:T(8,128)S(1)}, u32[]{:S(2)}, u32[]{:S(2)}) collective-permute-start(f32[24,16,256]{2,1,0:T(8,128)S(1)} %get-tuple-element.30), channel_id=1, source_target_pairs={{0,248},{8,0},{16,8},{24,16},{32,24},{40,32},{48,40},{56,48},{64,5... | collective-permute-start | bytes 1179656 | tf_op jit(solution)/shard_map/ppermute | solution.py:540
  16.6 5.6 %collective-permute-start.5 = (f32[24,128]{1,0:T(8,128)S(1)}, f32[24,128]{1,0:T(8,128)S(1)}, u32[]{:S(2)}, u32[]{:S(2)}) collective-permute-start(f32[24,128]{1,0:T(8,128)S(1)} %get-tuple-element.24.west), channel_id=1, source_target_pairs={{0,240},{8,248},{16,0},{24,8},{32,16},{40,24},{48,32},{56,40},{64,... | collective-permute-start | bytes 36872 | tf_op jit(solution)/shard_map/ppermute | solution.py:540
  20.3 7.3 %collective-permute-start.4 = (f32[24,128]{1,0:T(8,128)S(1)}, f32[24,128]{1,0:T(8,128)S(1)}, u32[]{:S(2)}, u32[]{:S(2)}) collective-permute-start(f32[24,128]{1,0:T(8,128)S(1)} %get-tuple-element.26.east), channel_id=1, source_target_pairs={{0,16},{8,24},{16,32},{24,40},{32,48},{40,56},{48,64},{56,72},{64,... | collective-permute-start | bytes 36872 | tf_op jit(solution)/shard_map/ppermute | solution.py:540
  28.8 6.6 %collective-permute-start.6 = (f32[248,256]{1,0:T(8,128)S(1)}, f32[248,256]{1,0:T(8,128)S(1)}, u32[]{:S(2)}, u32[]{:S(2)}) collective-permute-start(f32[248,256]{1,0:T(8,128)S(1)} %get-tuple-element.32.to_up), channel_id=1, source_target_pairs={{0,1},{1,2},{2,3},{3,4},{4,5},{5,6},{6,7},{7,0},{8,9},{9,10},{10,1... | collective-permute-start | bytes 761864 | tf_op jit(solution)/shard_map/ppermute | solution.py:540
  29.5 8.4 %collective-permute-start.7 = (f32[248,256]{1,0:T(8,128)S(1)}, f32[248,256]{1,0:T(8,128)S(1)}, u32[]{:S(2)}, u32[]{:S(2)}) collective-permute-start(f32[248,256]{1,0:T(8,128)S(1)} %get-tuple-element.33.to_down), channel_id=1, source_target_pairs={{0,7},{1,0},{2,1},{3,2},{4,3},{5,4},{6,5},{7,6},{8,15},{9,8},{10,9... | collective-permute-start | bytes 761864 | tf_op jit(solution)/shard_map/ppermute | solution.py:540

commit v5 on v4

--- a/solution.py
+++ b/solution.py
@@ -196,6 +196,7 @@
 Y_LEAD = 8
 Y_HELD = BX + 2
 Y_ROWS = Y_LEAD + 23 * Y_HELD + 10
+Y_SENT = Y_LEAD + 14 * Y_HELD + 12
 
 
 def put(n, x, shift):
@@ -263,11 +264,11 @@
 
 
 def y_faces(
-    ext_in, from_left, from_right, far_left, far_right, west, east, vel, solid,
-    ext, to_down, to_up,
-    items, where_xy, where_z, stack,
+    ext_in, from_left, from_right, far_left, far_right, west, east, vel, solid, after,
+    ext, to_down, to_up, send_down, send_up,
+    items, where_xy, where_z, stack, reads, part,
 ):
-    del ext_in
+    del ext_in, after
     gx, last = lax.axis_index("gx"), lax.axis_size("gx") - 1
     for n, (face, ok) in enumerate(((from_left, gx > 0), (from_right, gx < last))):
         lanes = slice(128 * n, 128 * n + 128)
@@ -292,7 +293,7 @@
             items, near, jnp.where(x == near_cell, y, -1), far, jnp.where(x == near_cell + sign, y, -1),
             cell % BZ, add, stack,
         )
-    for sign, out, near_y, far_y in ((1, to_down, 0, 1), (-1, to_up, BY - 1, BY - 2)):
+    for sign, out, send, near_y, far_y in ((1, to_down, send_down, 0, 1), (-1, to_up, send_up, BY - 1, BY - 2)):
         near, far = face_rows(1, sign)
         out[0:Y_LEAD, :] = jnp.zeros((Y_LEAD, BZ), F32)
         out[Y_ROWS - 10 : Y_ROWS, :] = jnp.zeros((10, BZ), F32)
@@ -308,6 +309,35 @@
             for axis in range(3):
                 out[put(19 + axis, x + 2, 0), :] = vel[axis, x, near_y : near_y + 1, :]
             out[put(22, x + 2, 0), :] = (solid[x, near_y : near_y + 1, :] > 0).astype(F32)
+        for i in range(19):
+            cx, cy, cz = VEL[i]
+            if cy == -sign:
+                reads[i] = jnp.zeros((16, BZ), F32)
+                continue
+            v = entry(out, 14 + far.index(i) if cy else near.index(i), cx)
+            if cx:
+                v = pltpu.roll(v, (-cx) % 16, 0)
+            reads[i] = shift_z(v, cz)
+
+        def keep(i, rows, lanes, value, far=far):
+            part[far.index(i), rows, lanes] = value
+
+        collide_block(
+            reads,
+            lambda axis, rows, lanes, out=out: entry(out, 19 + axis, 0)[rows, lanes],
+            lambda rows, lanes: jnp.zeros((8, 128), jnp.bool_),
+            far,
+            keep,
+        )
+        send[0:Y_LEAD, :] = jnp.zeros((Y_LEAD, BZ), F32)
+        send[Y_SENT - 12 : Y_SENT, :] = jnp.zeros((12, BZ), F32)
+        for slot, i in enumerate(far):
+            first, source = Y_LEAD + Y_HELD * slot, Y_LEAD + Y_HELD * near.index(i)
+            send[first : first + Y_HELD, :] = out[source : source + Y_HELD, :]
+            first = Y_LEAD + Y_HELD * (5 + slot)
+            send[first : first + Y_HELD, :] = part[slot, 1 : 1 + Y_HELD, :]
+        first, source = Y_LEAD + Y_HELD * 10, Y_LEAD + Y_HELD * 19
+        send[first : first + 4 * Y_HELD, :] = out[source : source + 4 * Y_HELD, :]
 
 
 def adjoint_collide(u, is_solid, r, want):
@@ -451,32 +481,32 @@
     in_down, in_up = gy > 0, gy < lax.axis_size("gy") - 1
     row = iota((8, 128), 0)
 
-    for ref, mine, near, far, mine_near, mine_far, sign, ok, out, y in (
-        (from_down, to_down, NEAR_DOWN, FAR_DOWN, NEAR_UP, FAR_UP, -1, in_down, low_face, 0),
-        (from_up, to_up, NEAR_UP, FAR_UP, NEAR_DOWN, FAR_DOWN, 1, in_up, high_face, BY - 1),
+    for ref, mine, far, mine_near, mine_far, sign, ok, out, y in (
+        (from_down, to_down, FAR_DOWN, NEAR_UP, FAR_UP, -1, in_down, low_face, 0),
+        (from_up, to_up, FAR_UP, NEAR_DOWN, FAR_DOWN, 1, in_up, high_face, BY - 1),
     ):
         for inside in (False, True):
             for i in range(19):
                 cx, cy, cz = VEL[i]
-                if inside:
-                    if cy == 0:
-                        v = entry(mine, mine_near[i], cx)
-                    elif cy == sign:
-                        v = jnp.where(ok, entry(ref, near[i], cx), 0.0)
-                    else:
-                        v = entry(mine, 14 + mine_far[i], cx)
-                elif cy == 0:
-                    v = entry(ref, near[i], cx)
-                elif cy == sign:
-                    v = entry(ref, 14 + far[i], cx)
+                if inside and cy == 0:
+                    v = entry(mine, mine_near[i], cx)
+                elif inside and cy == sign:
+                    v = jnp.where(ok, entry(ref, far[i], cx), 0.0)
+                elif inside:
+                    v = entry(mine, 14 + mine_far[i], cx)
+                elif cy == -sign:
+                    v = entry(mine, mine_near[i], cx)
                 else:
-                    v = entry(mine, mine_near[i], cx)
+                    reads[i] = jnp.zeros((16, BZ), F32)
+                    continue
                 if cx:
                     v = pltpu.roll(v, (-cx) % 16, 0)
                 reads[i] = shift_z(v, cz)
 
-            def keep_face(i, rows, lanes, value, out=out, far=far, ok=ok):
+            def keep_face(i, rows, lanes, value, ref=ref, out=out, far=far, ok=ok):
                 x = row + rows.start
+                sent = entry(ref, 5 + far[i], 0)[rows, lanes]
+                value = value + jnp.where(entry(ref, 13, 0)[rows, lanes] > 0.0, 0.0, sent)
                 good = ok & ((x > 1) | in_left) & ((x < EX - 2) | in_right)
                 out[far[i], rows, lanes] = jnp.where(good, value, 0.0)
 
@@ -493,11 +523,11 @@
                         one = jnp.where(in_right, one, 0.0)
                     mid[i, x, y : y + 1, lanes] = one
 
-            source = mine if inside else ref
+            source, first_entry = (mine, 19) if inside else (ref, 10)
             collide_block(
                 reads,
-                lambda axis, rows, lanes, source=source: entry(source, 19 + axis, 0)[rows, lanes],
-                lambda rows, lanes, source=source: entry(source, 22, 0)[rows, lanes] > 0.0,
+                lambda axis, rows, lanes, source=source, n=first_entry: entry(source, n + axis, 0)[rows, lanes],
+                lambda rows, lanes, source=source, n=first_entry: entry(source, n + 3, 0)[rows, lanes] > 0.0,
                 ALL if inside else face_rows(1, sign)[1],
                 keep_row if inside else keep_face,
             )
@@ -591,20 +621,21 @@
     from_right = in_vmem(shifted(to_left, "gx", -1))
     far_left = in_vmem(shifted(east, "gx", 2))
     far_right = in_vmem(shifted(west, "gx", -2))
-    ext, to_down, to_up = call(
+    y_message = pltpu.VMEM((Y_SENT, BZ), F32)
+    reads = pltpu.VMEM((19, BY, BZ), F32)
+    ext, to_down, to_up, send_down, send_up = call(
         y_faces,
-        (extended, y_face, y_face),
-        [vmem] * 9,
-        (ext, from_left, from_right, far_left, far_right, west, east, vel_late, solid_v),
+        (extended, y_face, y_face, y_message, y_message),
+        [vmem] * 10,
+        (ext, from_left, from_right, far_left, far_right, west, east, vel_late, solid_v, vel_early),
         scratch=[
             pltpu.VMEM((24, 256), F32), pltpu.VMEM((128, 256), bf16), pltpu.VMEM((BZ, 256), bf16),
-            pltpu.VMEM((608, 256), bf16),
+            pltpu.VMEM((608, 256), bf16), reads, pltpu.VMEM((5, 16, BZ), F32),
         ],
         aliases={0: 0},
     )
-    from_down = in_vmem(shifted(to_up, "gy", 1))
-    from_up = in_vmem(shifted(to_down, "gy", -1))
-    reads = pltpu.VMEM((19, BY, BZ), F32)
+    from_down = in_vmem(shifted(send_up, "gy", 1))
+    from_up = in_vmem(shifted(send_down, "gy", -1))
     mid = call(
         late_planes, extended, [vmem] * 5, (ext, from_left, from_right, vel_late, solid_v), scratch=[reads]
     )

time: 41.6 us -> 41 us (0.986)
  waiting for transfers between devices: 12.2 us -> 11.2 us
    ppermute x8, waiting for transfers between devices: 12.2 us -> 11.2 us  [shifted(): lax.ppermute(value, axis, [(i, (i + step) % count) for i in range(count)])]
where the time goes in v5:
time: 41 us; the launch traced here: 40.8 us
  Pallas kernels  14.7 us (36%)
  starting transfers between devices  14.2 us (35%)
  waiting for transfers between devices  11.2 us (27%)
  between operations  0.71 us (2%)
    pallas_call x8, Pallas kernels, call(): pl.pallas_call(body, out_shape=outs, in_specs=in_specs, out_specs=out_spe...  14.7 us
    ppermute x8, starting transfers between devices, shifted(): lax.ppermute(value, axis, [(i, (i + step) % count) for i in range(count)])  14.2 us
    ppermute x8, waiting for transfers between devices, shifted(): lax.ppermute(value, axis, [(i, (i + step) % count) for i in range(count)])  11.2 us
  transfers between devices with their start and end apart: 8, of which 4 were waited for; matrix products, arithmetic and copies ran while one was open for 0% of the time, Pallas kernels for 18%

profile of v5, /device:TPU:6, one launch (start us, length us, event | category | flops | bytes accessed | tf_op | source)
XLA Modules:
  0.0 40.8 jit_solution(14254436965826716301)
XLA Ops:
  0.6 1.3 %shard_map.87 = (f32[24,128]{1,0:T(8,128)S(1)}, f32[24,128]{1,0:T(8,128)S(1)}, f32[24,128]{1,0:T(8,128)S(1)}) custom-call(f32[19,128]{1,0:T(8,128)} %bitcast.8, s32[1,128]{1,0:T(1,128)} %bitcast.9, s32[1,128]{1,0:T(1,128)} %bitcast.10), custom_call_target="tpu_custom_call" | custom-call | tf_op jit(solution)/shard_map/pallas_call | solution.py:60
  2.0 1.6 %collective-permute-start = (f32[24,128]{1,0:T(8,128)S(1)}, f32[24,128]{1,0:T(8,128)S(1)}, u32[]{:S(2)}, u32[]{:S(2)}) collective-permute-start(f32[24,128]{1,0:T(8,128)S(1)} %get-tuple-element.22), channel_id=1, source_target_pairs={{0,1},{1,2},{2,3},{3,4},{4,5},{5,6},{6,7},{7,0},{8,9},{9,10},{10,1... | collective-permute-start | bytes 36872 | tf_op jit(solution)/shard_map/ppermute | solution.py:570
  3.5 0.5 %collective-permute-start.1 = (f32[24,128]{1,0:T(8,128)S(1)}, f32[24,128]{1,0:T(8,128)S(1)}, u32[]{:S(2)}, u32[]{:S(2)}) collective-permute-start(f32[24,128]{1,0:T(8,128)S(1)} %get-tuple-element.24), channel_id=1, source_target_pairs={{0,7},{1,0},{2,1},{3,2},{4,3},{5,4},{6,5},{7,6},{8,15},{9,8},{10,9... | collective-permute-start | bytes 36872 | tf_op jit(solution)/shard_map/ppermute | solution.py:570
  4.1 2.8 %shard_map.86 = (f32[3,8,16,256]{3,2,1,0:T(8,128)S(1)}, f32[19,12,16,256]{3,2,1,0:T(8,128)S(1)}, s32[8,16,256]{2,1,0:T(8,128)S(1)}) custom-call(bf16[2,19,8,16,256]{4,3,2,1,0:T(8,128)(2,1)} %pops.3, f32[2,8,32,19]{3,2,1,0:T(8,128)} %bitcast.6, f32[19,8,16,256]{3,2,1,0:T(8,128)} %adj.1, s32[8,16,256]{2,1,0:T(8,128)} %solid_in.1), custom_call_target="tpu_custom_call" | custom-call | tf_op jit(solution)/shard_map/pallas_call | solution.py:60
  6.9 0.0 collective-permute-done.below
  6.9 2.4 %collective-permute-done.1.above = f32[24,128]{1,0:T(8,128)S(1)} collective-permute-done((f32[24,128]{1,0:T(8,128)S(1)}, f32[24,128]{1,0:T(8,128)S(1)}, u32[]{:S(2)}, u32[]{:S(2)}) %collective-permute-start.1) | collective-permute-done | bytes 12320 | tf_op jit(solution)/shard_map/ppermute | solution.py:570
  9.3 0.1 shard_map.88
  9.4 0.8 %shard_map.89 = (f32[19,12,16,256]{3,2,1,0:T(8,128)S(1)}, f32[24,16,256]{2,1,0:T(8,128)S(1)}, f32[24,16,256]{2,1,0:T(8,128)S(1)}) custom-call(f32[19,12,16,256]{3,2,1,0:T(8,128)S(1)} %get-tuple-element.21.ext_in, f32[24,128]{1,0:T(8,128)S(1)} %get-tuple-element.26.west, f32[24,128]{1,0:T(8,128)S(1)} %get-tuple-element.27.here.after, ...), custom_call_target="tpu_custom_call", output_to_operand_aliasing={{0}: (0, {})} | custom-call | tf_op jit(solution)/shard_map/pallas_call | solution.py:60
  10.3 0.1 collective-permute-start.2
  10.4 6.3 %collective-permute-start.3 = (f32[24,16,256]{2,1,0:T(8,128)S(1)}, f32[24,16,256]{2,1,0:T(8,128)S(1)}, u32[]{:S(2)}, u32[]{:S(2)}) collective-permute-start(f32[24,16,256]{2,1,0:T(8,128)S(1)} %get-tuple-element.32), channel_id=1, source_target_pairs={{0,248},{8,0},{16,8},{24,16},{32,24},{40,32},{48,40},{56,48},{64,5... | collective-permute-start | bytes 1179656 | tf_op jit(solution)/shard_map/ppermute | solution.py:570
  16.6 3.6 %collective-permute-start.5 = (f32[24,128]{1,0:T(8,128)S(1)}, f32[24,128]{1,0:T(8,128)S(1)}, u32[]{:S(2)}, u32[]{:S(2)}) collective-permute-start(f32[24,128]{1,0:T(8,128)S(1)} %get-tuple-element.26.west), channel_id=1, source_target_pairs={{0,240},{8,248},{16,0},{24,8},{32,16},{40,24},{48,32},{56,40},{64,... | collective-permute-start | bytes 36872 | tf_op jit(solution)/shard_map/ppermute | solution.py:570
  20.3 0.0 collective-permute-start.4
  20.3 2.8 %shard_map.90.after.vel = f32[3,8,16,256]{3,2,1,0:T(8,128)S(1)} custom-call(bf16[2,19,8,16,256]{4,3,2,1,0:T(8,128)(2,1)} %pops.3, f32[2,8,32,19]{3,2,1,0:T(8,128)} %bitcast.7, f32[24,128]{1,0:T(8,128)S(1)} %get-tuple-element.27.here.after), custom_call_target="tpu_custom_call" | custom-call | tf_op jit(solution)/shard_map/pallas_call | solution.py:60
  23.1 0.0 collective-permute-done.5.far_right
  23.1 4.5 %collective-permute-done.4.far_left = f32[24,128]{1,0:T(8,128)S(1)} collective-permute-done((f32[24,128]{1,0:T(8,128)S(1)}, f32[24,128]{1,0:T(8,128)S(1)}, u32[]{:S(2)}, u32[]{:S(2)}) %collective-permute-start.4) | collective-permute-done | bytes 12320 | tf_op jit(solution)/shard_map/ppermute | solution.py:570
  27.6 0.0 collective-permute-done.2.from_left
  27.6 0.0 collective-permute-done.3.from_right
  27.6 1.6 %shard_map.91 = (f32[19,12,16,256]{3,2,1,0:T(8,128)S(1)}, f32[248,256]{1,0:T(8,128)S(1)}, f32[248,256]{1,0:T(8,128)S(1)}, f32[160,256]{1,0:T(8,128)S(1)}, f32[160,256]{1,0:T(8,128)S(1)}) custom-call(f32[19,12,16,256]{3,2,1,0:T(8,128)S(1)} %get-tuple-element.30.ext_in, ...), custom_call_target="tpu_custom_call", output_to_operand_aliasing={{0}: (0, {})} | custom-call | tf_op jit(solution)/shard_map/pallas_call | solution.py:60
  29.2 0.7 %collective-permute-start.6 = (f32[160,256]{1,0:T(8,128)S(1)}, f32[160,256]{1,0:T(8,128)S(1)}, u32[]{:S(2)}, u32[]{:S(2)}) collective-permute-start(f32[160,256]{1,0:T(8,128)S(1)} %get-tuple-element.34), channel_id=1, source_target_pairs={{0,1},{1,2},{2,3},{3,4},{4,5},{5,6},{6,7},{7,0},{8,9},{9,10},{10,1... | collective-permute-start | bytes 491528 | tf_op jit(solution)/shard_map/ppermute | solution.py:570
  29.9 1.4 %collective-permute-start.7 = (f32[160,256]{1,0:T(8,128)S(1)}, f32[160,256]{1,0:T(8,128)S(1)}, u32[]{:S(2)}, u32[]{:S(2)}) collective-permute-start(f32[160,256]{1,0:T(8,128)S(1)} %get-tuple-element.35), channel_id=1, source_target_pairs={{0,7},{1,0},{2,1},{3,2},{4,3},{5,4},{6,5},{7,6},{8,15},{9,8},{10,9... | collective-permute-start | bytes 491528 | tf_op jit(solution)/shard_map/ppermute | solution.py:570
  31.3 1.7 %shard_map.92.mid_in = f32[19,12,16,256]{3,2,1,0:T(8,128)S(1)} custom-call(f32[19,12,16,256]{3,2,1,0:T(8,128)S(1)} %get-tuple-element.33.ext, f32[24,16,256]{2,1,0:T(8,128)S(1)} %collective-permute-done.2.from_left, f32[24,16,256]{2,1,0:T(8,128)S(1)} %collective-permute-done.3.from_right, f32[3,8,16,256]{3,2,1,0:T(8,128)S(1)} %get-tuple-element.29.vel, ...), custom_call_target="tpu_custom_call" | custom-call | tf_op jit(solution)/shard_map/pallas_call | solution.py:60
  33.0 1.6 %collective-permute-done.6.from_down = f32[160,256]{1,0:T(8,128)S(1)} collective-permute-done((f32[160,256]{1,0:T(8,128)S(1)}, f32[160,256]{1,0:T(8,128)S(1)}, u32[]{:S(2)}, u32[]{:S(2)}) %collective-permute-start.6) | collective-permute-done | bytes 163872 | tf_op jit(solution)/shard_map/ppermute | solution.py:570
  34.6 2.7 %collective-permute-done.7.from_up = f32[160,256]{1,0:T(8,128)S(1)} collective-permute-done((f32[160,256]{1,0:T(8,128)S(1)}, f32[160,256]{1,0:T(8,128)S(1)}, u32[]{:S(2)}, u32[]{:S(2)}) %collective-permute-start.7) | collective-permute-done | bytes 163872 | tf_op jit(solution)/shard_map/ppermute | solution.py:570
  37.3 3.5 %shard_map.93 = (f32[19,8,16,256]{3,2,1,0:T(8,128)}, f32[19,8,16,256]{3,2,1,0:T(8,128)}, f32[19,12,16,256]{3,2,1,0:T(8,128)S(1)}) custom-call(f32[19,12,16,256]{3,2,1,0:T(8,128)S(1)} %shard_map.92.mid_in, f32[160,256]{1,0:T(8,128)S(1)} %collective-permute-done.6.from_down, ...), custom_call_target="tpu_custom_call", output_to_operand_aliasing={{2}: (0, {})} | custom-call | tf_op jit(solution)/shard_map/pallas_call | solution.py:60
Async XLA Ops:
  2.0 4.9 %collective-permute-start = (f32[24,128]{1,0:T(8,128)S(1)}, f32[24,128]{1,0:T(8,128)S(1)}, u32[]{:S(2)}, u32[]{:S(2)}) collective-permute-start(f32[24,128]{1,0:T(8,128)S(1)} %get-tuple-element.22), channel_id=1, source_target_pairs={{0,1},{1,2},{2,3},{3,4},{4,5},{5,6},{6,7},{7,0},{8,9},{9,10},{10,1... | collective-permute-start | bytes 36872 | tf_op jit(solution)/shard_map/ppermute | solution.py:570
  3.5 5.8 %collective-permute-start.1 = (f32[24,128]{1,0:T(8,128)S(1)}, f32[24,128]{1,0:T(8,128)S(1)}, u32[]{:S(2)}, u32[]{:S(2)}) collective-permute-start(f32[24,128]{1,0:T(8,128)S(1)} %get-tuple-element.24), channel_id=1, source_target_pairs={{0,7},{1,0},{2,1},{3,2},{4,3},{5,4},{6,5},{7,6},{8,15},{9,8},{10,9... | collective-permute-start | bytes 36872 | tf_op jit(solution)/shard_map/ppermute | solution.py:570
  10.3 17.3 %collective-permute-start.2 = (f32[24,16,256]{2,1,0:T(8,128)S(1)}, f32[24,16,256]{2,1,0:T(8,128)S(1)}, u32[]{:S(2)}, u32[]{:S(2)}) collective-permute-start(f32[24,16,256]{2,1,0:T(8,128)S(1)} %get-tuple-element.31), channel_id=1, source_target_pairs={{0,8},{8,16},{16,24},{24,32},{32,40},{40,48},{48,56},{56,64},{64,7... | collective-permute-start | bytes 1179656 | tf_op jit(solution)/shard_map/ppermute | solution.py:570
  10.4 17.2 %collective-permute-start.3 = (f32[24,16,256]{2,1,0:T(8,128)S(1)}, f32[24,16,256]{2,1,0:T(8,128)S(1)}, u32[]{:S(2)}, u32[]{:S(2)}) collective-permute-start(f32[24,16,256]{2,1,0:T(8,128)S(1)} %get-tuple-element.32), channel_id=1, source_target_pairs={{0,248},{8,0},{16,8},{24,16},{32,24},{40,32},{48,40},{56,48},{64,5... | collective-permute-start | bytes 1179656 | tf_op jit(solution)/shard_map/ppermute | solution.py:570
  16.6 6.5 %collective-permute-start.5 = (f32[24,128]{1,0:T(8,128)S(1)}, f32[24,128]{1,0:T(8,128)S(1)}, u32[]{:S(2)}, u32[]{:S(2)}) collective-permute-start(f32[24,128]{1,0:T(8,128)S(1)} %get-tuple-element.26.west), channel_id=1, source_target_pairs={{0,240},{8,248},{16,0},{24,8},{32,16},{40,24},{48,32},{56,40},{64,... | collective-permute-start | bytes 36872 | tf_op jit(solution)/shard_map/ppermute | solution.py:570
  20.3 7.3 %collective-permute-start.4 = (f32[24,128]{1,0:T(8,128)S(1)}, f32[24,128]{1,0:T(8,128)S(1)}, u32[]{:S(2)}, u32[]{:S(2)}) collective-permute-start(f32[24,128]{1,0:T(8,128)S(1)} %get-tuple-element.28.east), channel_id=1, source_target_pairs={{0,16},{8,24},{16,32},{24,40},{32,48},{40,56},{48,64},{56,72},{64,... | collective-permute-start | bytes 36872 | tf_op jit(solution)/shard_map/ppermute | solution.py:570
  29.2 5.4 %collective-permute-start.6 = (f32[160,256]{1,0:T(8,128)S(1)}, f32[160,256]{1,0:T(8,128)S(1)}, u32[]{:S(2)}, u32[]{:S(2)}) collective-permute-start(f32[160,256]{1,0:T(8,128)S(1)} %get-tuple-element.34), channel_id=1, source_target_pairs={{0,1},{1,2},{2,3},{3,4},{4,5},{5,6},{6,7},{7,0},{8,9},{9,10},{10,1... | collective-permute-start | bytes 491528 | tf_op jit(solution)/shard_map/ppermute | solution.py:570
  29.9 7.4 %collective-permute-start.7 = (f32[160,256]{1,0:T(8,128)S(1)}, f32[160,256]{1,0:T(8,128)S(1)}, u32[]{:S(2)}, u32[]{:S(2)}) collective-permute-start(f32[160,256]{1,0:T(8,128)S(1)} %get-tuple-element.35), channel_id=1, source_target_pairs={{0,7},{1,0},{2,1},{3,2},{4,3},{5,4},{6,5},{7,6},{8,15},{9,8},{10,9... | collective-permute-start | bytes 491528 | tf_op jit(solution)/shard_map/ppermute | solution.py:570
